TPU v7x, 256 devices: a whole 4x4x8 slice. The times are simulated.
256 devices in a mesh: gx: 8 (over x, z_lo), gy: 4 (over z_hi), ta: 8 (over y, core).
Axes of the slice: x: 4, y: 4, z: 8 (z_hi: 4, z_lo: 2; z = z_hi * 2 + z_lo), core: 2. Of those that a mesh axis runs over, the one named last changes fastest.
Arguments:
- traces: bfloat16 [1048576, 1024], P(('gx', 'gy'), 'ta'), may hold values from -6 to 6
- interp: bfloat16 [2, 16], replicated, may hold values from -1.5 to 1.5
- translations: bfloat16 [4, 2048, 1024], P(None, ('gx', 'gy')), may hold values from -0.125 to 0.125
- leaf_slot: int32 [65536], P(('gx', 'gy', 'ta')), may hold values from 0 to 255, as said below
- pairing: int32 [4, 65536], P(None, ('gx', 'gy', 'ta')), may hold values from 0 to 255, as said below
Outputs:
- coefficients: bfloat16 [65536, 1024], P(('gx', 'gy', 'ta'))
Inputs may be any that keep to these rules, and one draw needn't show every extreme that they name: `leaf_slot`: each aligned block of 256 entries (the leaves of one device) is a permutation of 0 to 255. `pairing`: for every level, each aligned block of 256 entries along the leaves is a permutation of 0 to 255.
All inputs are finite; a program needn't handle non-finite values.
Results may differ from a plain program's by a relative error of at most 0.0082.
Values may be sent and summed in bfloat16 or wider, within the bound.
No kernel may reach another device: no remote copies, remote signals or barrier semaphores. Data moves between devices by JAX's collectives and lax.ppermute only.
A program may use at most 128 MiB of HBM per device.

v0:
```python
import math

import jax
import jax.numpy as jnp
from jax import lax
from jax.sharding import Mesh
from jax.sharding import PartitionSpec as P

NF = 256
CHEB = 2
BOXT = 16
GX_GY = ("gx_0", "gx_1", "gy")
GX_GY_TA = ("gx_0", "gx_1", "gy", "ta")


def whole_of(x, axes, dim):
    if not axes:
        return x
    nearer = lax.all_gather(x, axes[-1], axis=dim, tiled=True)
    return whole_of(nearer, axes[:-1], dim)


def from_partner(value, axis, bit):
    mask = 2**bit
    pairs = [(source, source ^ mask) for source in range(lax.axis_size(axis))]
    return lax.ppermute(value, axis, pairs)


def spectrum_table(length, count):
    sample_pos = lax.broadcasted_iota(jnp.float32, (length, count), 0)
    frequency = lax.broadcasted_iota(jnp.float32, (length, count), 1) + 1.0
    angles = 2.0 * math.pi / length * jnp.mod(sample_pos * frequency, float(length))
    factor = math.sqrt(2.0 / length)
    return jnp.concatenate([jnp.cos(angles) * factor, -jnp.sin(angles) * factor], axis=1).astype(
        jnp.bfloat16
    )


def move_boxes(blocks):
    return lax.all_to_all(blocks, GX_GY, split_axis=0, concat_axis=0, tiled=True)


def on_device(traces, interp, translations, leaf_slot, pairing):
    local_boxes = traces.shape[0] // BOXT
    local_cols = traces.shape[1]
    sampled_local = jnp.einsum(
        "cb,kbt->kct",
        interp,
        traces.reshape(local_boxes, BOXT, local_cols),
        preferred_element_type=jnp.float32,
    )
    sampled_local = sampled_local.astype(jnp.bfloat16).reshape(local_boxes * CHEB, local_cols)
    sampled = lax.all_to_all(sampled_local, "ta", split_axis=0, concat_axis=1, tiled=True)
    sample_count = sampled.shape[1]
    box_count = sampled.shape[0] // CHEB
    fourier = spectrum_table(sample_count, NF)
    spectra = jnp.dot(sampled, fourier, preferred_element_type=jnp.float32)
    cheb_points = spectra.astype(jnp.bfloat16).reshape(box_count, CHEB * 2 * NF)
    arrived = move_boxes(cheb_points)
    states = jnp.take(arrived, leaf_slot, axis=0)
    log_devices = lax.axis_size(GX_GY_TA).bit_length() - 1
    level_count = translations.shape[0]
    every_level = whole_of(translations, GX_GY, 1)
    for layer_index in range(level_count):
        flip_bit = layer_index * log_devices // level_count
        partner = from_partner(states, GX_GY_TA, flip_bit)
        aligned = jnp.take(partner, pairing[layer_index], axis=0)
        joined = jnp.concatenate([states, aligned], axis=1)
        product_sum = jnp.dot(joined, every_level[layer_index], preferred_element_type=jnp.float32)
        states = product_sum.astype(jnp.bfloat16)
    return states


def solution(mesh):
    split = Mesh(
        mesh.devices.reshape(4, 2, mesh.shape["gy"], mesh.shape["ta"]), ("gx_0", "gx_1", "gy", "ta")
    )
    placed = (P(GX_GY, "ta"), P(), P(None, GX_GY, None), P(GX_GY_TA), P(None, GX_GY_TA))
    return jax.shard_map(
        on_device, mesh=split, in_specs=placed, out_specs=P(GX_GY_TA, None), check_vma=False
    )
```

profile of v0, /device:TPU:2, one launch (start us, length us, event | category | flops | bytes accessed | tf_op | source)
XLA Modules:
  0.0 367.2 jit_solution(10943753191328452643)
XLA Ops:
  6.5 0.0 copy-start
  6.5 0.0 all-gather.4.cloned.1.call-start
  6.5 0.7 all-gather.4.cloned.1.call-update
  7.3 0.0 all-gather.6.cloned.1.call-start
  7.3 56.6 %all-gather.4.cloned.1.call-done = bf16[4,256,1024]{2,1,0:T(8,128)(2,1)} async-done(((bf16[4,64,1024]{2,1,0:T(8,128)(2,1)}), bf16[4,256,1024]{2,1,0:T(8,128)(2,1)}) %all-gather.4.cloned.1.call-update) | async-done | bytes 2097168 | tf_op jit(solution)/shard_map/all_gather | solution.py:19
  63.9 0.0 all-gather.6.cloned.1.call-update
  64.0 0.0 all-gather.8.cloned.1.call-start
  64.0 61.9 %all-gather.6.cloned.1.call-done = bf16[4,512,1024]{2,1,0:T(8,128)(2,1)} async-done(((bf16[4,256,1024]{2,1,0:T(8,128)(2,1)}), bf16[4,512,1024]{2,1,0:T(8,128)(2,1)}) %all-gather.6.cloned.1.call-update) | async-done | bytes 4194320 | tf_op jit(solution)/shard_map/all_gather | solution.py:19
  125.9 0.0 all-gather.8.cloned.1.call-update
  125.9 0.0 copy-done
  125.9 4.6 %convolution_convert_fusion = bf16[2048,128,2]{1,2,0:T(2,128)(2,1)S(1)} fusion(bf16[2048,16,128]{2,1,0:T(8,128)(2,1)} %bitcast.38, bf16[2,16]{1,0:T(2,128)(2,1)S(1)} %copy-done), kind=kOutput, calls=%fused_computation.14 | convolution fusion | flops 17301504 | bytes 9437248 | tf_op jit(solution)/shard_map/cb,kbt->kct/dot_general | solution.py:46
  130.5 1.3 copy.6
  131.8 4.3 %all-to-all-start = ((bf16[8,512,128]{1,2,0:T(8,128)(2,1)}), bf16[8,512,128]{1,2,0:T(8,128)(2,1)S(1)}, u32[]{:S(2)}, u32[]{:S(2)}) async-start(bf16[8,512,128]{1,2,0:T(8,128)(2,1)} %copy.6), calls=%async_computation | async-start | bytes 2097152 | tf_op jit(solution)/shard_map/all_to_all | solution.py:53
  136.1 4.8 %multiply_convert_fusion.1 = (bf16[1024,256]{1,0:T(8,128)(2,1)S(1)}, bf16[1024,256]{1,0:T(8,128)(2,1)S(1)}) fusion(f32[256]{0:T(256)S(1)} %iota_add_fusion), kind=kLoop, calls=%fused_computation.37 | loop fusion | flops 3407872 | bytes 1049600 | tf_op jit(solution)/shard_map/convert
  140.9 0.0 copy-start.2
  140.9 0.0 copy-start.1
  140.9 11.2 %all-to-all-done = bf16[8,512,128]{1,2,0:T(8,128)(2,1)S(1)} async-done(((bf16[8,512,128]{1,2,0:T(8,128)(2,1)}), bf16[8,512,128]{1,2,0:T(8,128)(2,1)S(1)}, u32[]{:S(2)}, u32[]{:S(2)}) %all-to-all-start) | async-done | bytes 1048608 | tf_op jit(solution)/shard_map/all_to_all | solution.py:53
  152.1 0.7 convolution_convert_fusion.1
  152.8 1.0 all_to_all.26
  153.8 9.2 %all-to-all-start.1 = ((bf16[32,8,1024]{2,1,0:T(8,128)(2,1)}), bf16[32,8,1024]{2,1,0:T(8,128)(2,1)S(1)}, u32[]{:S(2)}, u32[]{:S(2)}) async-start(bf16[32,8,1024]{2,1,0:T(8,128)(2,1)} %all_to_all.26), calls=%async_computation.1 | async-start | bytes 1048576 | tf_op jit(solution)/shard_map/all_to_all | solution.py:40
  163.0 0.0 copy-done.2
  163.1 0.0 copy-done.1
  163.1 15.5 %all-to-all-done.1 = bf16[32,8,1024]{2,1,0:T(8,128)(2,1)S(1)} async-done(((bf16[32,8,1024]{2,1,0:T(8,128)(2,1)}), bf16[32,8,1024]{2,1,0:T(8,128)(2,1)S(1)}, u32[]{:S(2)}, u32[]{:S(2)}) %all-to-all-start.1) | async-done | bytes 524320 | tf_op jit(solution)/shard_map/all_to_all | solution.py:40
  178.6 1.2 gather_fusion
  179.8 0.1 broadcast_select_fusion.4
  179.9 0.1 collective-permute-start
  180.0 1.9 collective-permute-done
  181.9 1.2 gather_fusion.1
  183.1 0.1 broadcast_select_fusion.3
  183.2 107.2 %all-gather.8.cloned.1.call-done = bf16[4,2048,1024]{2,1,0:T(8,128)(2,1)} async-done(((bf16[4,512,1024]{2,1,0:T(8,128)(2,1)}), bf16[4,2048,1024]{2,1,0:T(8,128)(2,1)}) %all-gather.8.cloned.1.call-update) | async-done | bytes 16777232 | tf_op jit(solution)/shard_map/all_gather | solution.py:19
  290.4 3.4 fusion.4
  293.8 3.1 collective-permute-start.1
  296.9 12.1 %collective-permute-done.1 = bf16[256,1024]{1,0:T(8,128)(2,1)S(1)} collective-permute-done((bf16[256,1024]{1,0:T(8,128)(2,1)S(1)}, bf16[256,1024]{1,0:T(8,128)(2,1)S(1)}, u32[]{:S(2)}, u32[]{:S(2)}) %collective-permute-start.1) | collective-permute-done | bytes 524320 | tf_op jit(solution)/shard_map/ppermute | solution.py:26
  309.0 1.2 gather_fusion.2
  310.2 0.1 broadcast_select_fusion.2
  310.3 3.5 fusion.5
  313.8 5.8 %collective-permute-start.2 = (bf16[256,1024]{1,0:T(8,128)(2,1)S(1)}, bf16[256,1024]{1,0:T(8,128)(2,1)S(1)}, u32[]{:S(2)}, u32[]{:S(2)}) collective-permute-start(bf16[256,1024]{1,0:T(8,128)(2,1)S(1)} %fusion.5), channel_id=1, source_target_pairs={{0,16},{1,17},{2,18},{3,19},{4,20},{5,21},{6,22},{7,23},{8,24},{9,... | collective-permute-start | bytes 1572872 | tf_op jit(solution)/shard_map/ppermute | solution.py:26
  319.6 21.5 %collective-permute-done.2 = bf16[256,1024]{1,0:T(8,128)(2,1)S(1)} collective-permute-done((bf16[256,1024]{1,0:T(8,128)(2,1)S(1)}, bf16[256,1024]{1,0:T(8,128)(2,1)S(1)}, u32[]{:S(2)}, u32[]{:S(2)}) %collective-permute-start.2) | collective-permute-done | bytes 524320 | tf_op jit(solution)/shard_map/ppermute | solution.py:26
  341.1 1.2 gather_fusion.3
  342.3 0.1 broadcast_select_fusion.1
  342.4 3.5 fusion.6
  345.9 0.7 collective-permute-start.3
  346.6 8.6 %collective-permute-done.3 = bf16[256,1024]{1,0:T(8,128)(2,1)S(1)} collective-permute-done((bf16[256,1024]{1,0:T(8,128)(2,1)S(1)}, bf16[256,1024]{1,0:T(8,128)(2,1)S(1)}, u32[]{:S(2)}, u32[]{:S(2)}) %collective-permute-start.3) | collective-permute-done | bytes 524320 | tf_op jit(solution)/shard_map/ppermute | solution.py:26
  355.2 1.2 gather_fusion.4
  356.3 0.1 broadcast_select_fusion
  356.4 4.2 %fusion.7 = bf16[256,1024]{1,0:T(8,128)(2,1)} fusion(bf16[4,2048,1024]{2,1,0:T(8,128)(2,1)} %all-gather.8.cloned.1.call-done, bf16[256,1024]{1,0:T(8,128)(2,1)S(1)} %broadcast_select_fusion, bf16[256,1024]{1,0:T(8,128)(2,1)S(1)} %fusion.6), kind=kOutput, calls=%fused_computation.18 | convolution fusion | flops 1076101120 | bytes 5767168 | tf_op jit(solution)/shard_map/dot_general | solution.py:69
  (17 shorter events, 0.1 us)
Async XLA Ops:
  6.5 119.3 %copy-start = (bf16[2,16]{1,0:T(2,128)(2,1)S(1)}, bf16[2,16]{1,0:T(2,128)(2,1)}, u32[]{:S(2)}) copy-start(bf16[2,16]{1,0:T(2,128)(2,1)} %param.8) | copy-start | bytes 196
  6.5 57.4 %all-gather.4.cloned.1.call-start = ((), (), s32[]{:S(2)}) async-start(), calls=%async_computation.2 | async-start | bytes 2621440 | tf_op jit(solution)/shard_map/all_gather | solution.py:19
  7.3 118.6 %all-gather.6.cloned.1.call-start = ((), (), s32[]{:S(2)}) async-start(), calls=%async_computation.3 | async-start | bytes 6291456 | tf_op jit(solution)/shard_map/all_gather | solution.py:19
  64.0 226.4 %all-gather.8.cloned.1.call-start = ((), (), s32[]{:S(2)}) async-start(), calls=%async_computation.4 | async-start | bytes 20971520 | tf_op jit(solution)/shard_map/all_gather | solution.py:19
  131.8 20.3 %all-to-all-start = ((bf16[8,512,128]{1,2,0:T(8,128)(2,1)}), bf16[8,512,128]{1,2,0:T(8,128)(2,1)S(1)}, u32[]{:S(2)}, u32[]{:S(2)}) async-start(bf16[8,512,128]{1,2,0:T(8,128)(2,1)} %copy.6), calls=%async_computation | async-start | bytes 2097152 | tf_op jit(solution)/shard_map/all_to_all | solution.py:53
  140.9 22.1 %copy-start.2 = (s32[256]{0:T(256)S(1)}, s32[256]{0:T(256)}, u32[]{:S(2)}) copy-start(s32[256]{0:T(256)} %param.10) | copy-start | bytes 3076
  140.9 22.2 %copy-start.1 = (s32[4,256]{1,0:T(4,128)S(1)}, s32[4,256]{1,0:T(4,128)}, u32[]{:S(2)}) copy-start(s32[4,256]{1,0:T(4,128)} %param.11) | copy-start | bytes 12292
  153.8 24.8 %all-to-all-start.1 = ((bf16[32,8,1024]{2,1,0:T(8,128)(2,1)}), bf16[32,8,1024]{2,1,0:T(8,128)(2,1)S(1)}, u32[]{:S(2)}, u32[]{:S(2)}) async-start(bf16[32,8,1024]{2,1,0:T(8,128)(2,1)} %all_to_all.26), calls=%async_computation.1 | async-start | bytes 1048576 | tf_op jit(solution)/shard_map/all_to_all | solution.py:40
  179.9 2.0 collective-permute-start
  293.8 15.2 %collective-permute-start.1 = (bf16[256,1024]{1,0:T(8,128)(2,1)S(1)}, bf16[256,1024]{1,0:T(8,128)(2,1)S(1)}, u32[]{:S(2)}, u32[]{:S(2)}) collective-permute-start(bf16[256,1024]{1,0:T(8,128)(2,1)S(1)} %fusion.4), channel_id=1, source_target_pairs={{0,4},{1,5},{2,6},{3,7},{4,0},{5,1},{6,2},{7,3},{8,12},{9,13},{10,... | collective-permute-start | bytes 1572872 | tf_op jit(solution)/shard_map/ppermute | solution.py:26
  313.8 27.3 %collective-permute-start.2 = (bf16[256,1024]{1,0:T(8,128)(2,1)S(1)}, bf16[256,1024]{1,0:T(8,128)(2,1)S(1)}, u32[]{:S(2)}, u32[]{:S(2)}) collective-permute-start(bf16[256,1024]{1,0:T(8,128)(2,1)S(1)} %fusion.5), channel_id=1, source_target_pairs={{0,16},{1,17},{2,18},{3,19},{4,20},{5,21},{6,22},{7,23},{8,24},{9,... | collective-permute-start | bytes 1572872 | tf_op jit(solution)/shard_map/ppermute | solution.py:26
  345.9 9.3 %collective-permute-start.3 = (bf16[256,1024]{1,0:T(8,128)(2,1)S(1)}, bf16[256,1024]{1,0:T(8,128)(2,1)S(1)}, u32[]{:S(2)}, u32[]{:S(2)}) collective-permute-start(bf16[256,1024]{1,0:T(8,128)(2,1)S(1)} %fusion.6), channel_id=1, source_target_pairs={{0,64},{1,65},{2,66},{3,67},{4,68},{5,69},{6,70},{7,71},{8,72},{9,... | collective-permute-start | bytes 1572872 | tf_op jit(solution)/shard_map/ppermute | solution.py:26
Sparse Core Ops, SparseCore 0:
  9.2 54.7 all-gather.3
  65.7 60.0 all-gather.5
  127.7 162.6 all-gather.7
where the time goes:
time: 372 us; the launch traced here: 367 us
  waiting for transfers between devices  297 us (80%)
  starting transfers between devices  23.2 us (6%)
  matrix products  19.9 us (5%)
  between operations  13.3 us (4%)
  local copies, waits for them, and re-layouts  8.12 us (2%)
  other arithmetic  5.44 us (1%)
    all_gather x3, waiting for transfers between devices, whole_of(): nearer = lax.all_gather(x, axes[-1], axis=dim, tiled=True)  226 us
    ppermute x4, waiting for transfers between devices, from_partner(): return lax.ppermute(value, axis, pairs)  44.1 us
    all_to_all x1, waiting for transfers between devices, move_boxes(): lax.all_to_all(blocks, GX_GY, split_axis=0, concat_axis=0, tiled=True)  15.5 us
    dot_general x4, matrix products, on_device(): jnp.dot(joined, every_level[layer_index], preferred_element_type=jnp.floa...  14.6 us
    all_to_all x1, waiting for transfers between devices, on_device(): lax.all_to_all(sampled_local, 'ta', split_axis=0, concat_axis=1, tiled=True)  11.2 us
    ppermute x4, starting transfers between devices, from_partner(): return lax.ppermute(value, axis, pairs)  9.64 us
    all_to_all x1, starting transfers between devices, move_boxes(): lax.all_to_all(blocks, GX_GY, split_axis=0, concat_axis=0, tiled=True)  9.24 us
  transfers between devices with their start and end apart: 9, of which 9 were waited for; matrix products, arithmetic and copies ran while one was open for 4% of the time, Pallas kernels for 0%

commit v1 on v0

v1 whole, which is shorter than its diff:
```python
import functools
import math

import jax
import jax.numpy as jnp
from jax import lax
from jax.experimental import pallas as pl
from jax.experimental.pallas import tpu as pltpu
from jax.sharding import Mesh
from jax.sharding import PartitionSpec as P

NF = 256
CHEB = 2
BOXT = 16
AXES = ("x", "zl", "zh", "y", "c")
GROUP = ("x", "zl", "zh")
TA = ("y", "c")
BF16 = jnp.bfloat16
F32 = jnp.float32
VMEM_LIMIT = 12 << 20
SHORT = 1 << 28
LONG = 1 << 37


def spectrum_table(length, count):
    step = 32
    frequency = lax.broadcasted_iota(jnp.int32, (step, count), 1) + 1
    digit = lax.broadcasted_iota(jnp.int32, (step, count), 0)
    low = (2.0 * math.pi / length) * ((digit * frequency) % length).astype(F32)
    high = (2.0 * math.pi / length) * ((digit * step * frequency) % length).astype(F32)
    factor = math.sqrt(2.0 / length)
    cos_low, sin_low = jnp.cos(low)[None], jnp.sin(low)[None]
    cos_high, sin_high = (jnp.cos(high) * factor)[:, None], (jnp.sin(high) * factor)[:, None]
    real = (cos_high * cos_low - sin_high * sin_low).reshape(length, count)
    imag = (sin_high * cos_low + cos_high * sin_low).reshape(length, count)
    return jnp.concatenate([real, -imag], axis=1).astype(BF16)


def flip(value, mask):
    size = lax.axis_size(AXES)
    return lax.ppermute(value, AXES, [(i, i ^ mask) for i in range(size)])


def shifted(value, axis, k):
    size = lax.axis_size(axis)
    return lax.ppermute(value, axis, [(i, (i + k) % size) for i in range(size)])


def pieces_from(value, axis):
    size = lax.axis_size(axis)
    away = {k: shifted(value, axis, k) for k in (2, 1, 3)}
    return [value if k == 0 else away[k] for k in range(size)]


def doubled(value, mask, bit):
    there = flip(value, mask)
    low = jnp.where(bit == 0, value, there)
    high = jnp.where(bit == 0, there, value)
    return jnp.concatenate([low, high], axis=0)


def select_rows(index, values):
    rows = values.shape[0]
    picks = lax.broadcasted_iota(jnp.int32, (index.shape[0], rows), 1) == index
    hot = jnp.where(picks, 1.0, 0.0).astype(BF16)
    return jnp.dot(hot, values, preferred_element_type=F32).astype(BF16)


def plan_copies(layout, place, mine, other, weights):
    x, y, c = place[0], place[1], place[2]
    copies = []
    for half, source in enumerate((mine, other)):
        column = jnp.where(c == half, 0, 512)
        for k in range(4):
            rows = pl.ds(pl.multiple_of(lax.rem(x + (4 - k), 4) * 512, 512), 512)
            if layout == "x":
                cols = pl.ds(pl.multiple_of(column, 512), 512)
                copies.append((source.at[k], weights.at[rows, cols]))
            else:
                for j in range(4):
                    cols = pl.ds(pl.multiple_of(column + lax.rem(y + (4 - j), 4) * 128, 128), 128)
                    copies.append((source.at[j, k], weights.at[rows, cols]))
    return copies


def near_body(layout, place, own, mine, other, weights, partial, sems):
    started = []
    for n, (source, target) in enumerate(plan_copies(layout, place, mine, other, weights)):
        copy = pltpu.make_async_copy(source, target, sems.at[n])
        copy.start()
        started.append(copy)
    for copy in started:
        copy.wait()
    for n in range(4):
        cols = slice(n * 256, (n + 1) * 256)
        partial[:, cols] = jnp.dot(own[...], weights[:1024, cols], preferred_element_type=F32)


def far_body(index, far, weights, partial, out):
    aligned = select_rows(index[...], far[...])
    for n in range(4):
        cols = slice(n * 256, (n + 1) * 256)
        total = jnp.dot(aligned, weights[1024:, cols], preferred_element_type=F32)
        out[:, cols] = (total + partial[:, cols]).astype(BF16)


def select_body(index, values, out):
    out[...] = select_rows(index[...], values[...])


def spectrum_body(sampled, table, out):
    out[...] = jnp.dot(sampled[...], table[...], preferred_element_type=F32).astype(BF16)


VMEM = pl.BlockSpec(memory_space=pltpu.VMEM)
HBM = pl.BlockSpec(memory_space=pltpu.HBM)


def on_chip(body, shape, flops, name, *operands):
    return pl.pallas_call(
        body,
        out_shape=jax.ShapeDtypeStruct(shape, BF16),
        in_specs=[VMEM] * len(operands),
        out_specs=VMEM,
        compiler_params=pltpu.CompilerParams(vmem_limit_bytes=VMEM_LIMIT),
        cost_estimate=pl.CostEstimate(flops=flops, bytes_accessed=1 << 20, transcendentals=0),
        name=name,
    )(*operands)


def near_step(level, layout, place, own, mine):
    other = flip(mine, 1)
    mine, other = [pltpu.with_memory_space_constraint(piece, pltpu.HBM) for piece in (mine, other)]
    return pl.pallas_call(
        functools.partial(near_body, layout),
        out_shape=[jax.ShapeDtypeStruct((2048, 1024), BF16), jax.ShapeDtypeStruct(own.shape, F32)],
        in_specs=[pl.BlockSpec(memory_space=pltpu.SMEM), VMEM, HBM, HBM],
        out_specs=[VMEM, VMEM],
        scratch_shapes=[pltpu.SemaphoreType.DMA((8 if layout == "x" else 32,))],
        compiler_params=pltpu.CompilerParams(vmem_limit_bytes=VMEM_LIMIT),
        cost_estimate=pl.CostEstimate(flops=256 * 2048 * 1024, bytes_accessed=6 << 20, transcendentals=0),
        name="near" + str(level),
    )(place, own, mine, other)


def far_step(level, index, far, joined, partial):
    return on_chip(far_body, far.shape, 256 * 2048 * 1024, "far" + str(level), index, far, joined, partial)


def on_device(traces, interp, translations, leaf_slot, pairing):
    x, y, c = lax.axis_index("x"), lax.axis_index("y"), lax.axis_index("c")
    zl, zh = lax.axis_index("zl"), lax.axis_index("zh")
    together = lax.optimization_barrier
    place = jnp.stack([x, y, c]).astype(jnp.int32)

    def column(values):
        return values.reshape(values.shape[0], 1)

    def half(level):
        return lax.dynamic_slice_in_dim(translations[level], c * 512, 512, 1)

    def eighth(level):
        return lax.dynamic_slice_in_dim(translations[level], c * 512 + y * 128, 128, 1)

    rows = doubled(jnp.concatenate([half(0), eighth(1), eighth(3), half(2)], axis=1), 8, zh % 2)
    early, late = rows[:, :768], rows[:, 768:]
    local_boxes = traces.shape[0] // BOXT
    local_cols = traces.shape[1]
    sampled = jnp.einsum(
        "cb,kbt->kct", interp, traces.reshape(local_boxes, BOXT, local_cols), preferred_element_type=F32
    )
    sampled = sampled.astype(BF16).reshape(local_boxes * CHEB, local_cols)
    sampled, early, late = together((sampled, early, late))

    sampled = lax.all_to_all(sampled, TA, split_axis=0, concat_axis=1, tiled=True)
    early = doubled(doubled(early, 16, zh // 2), 32, zl)
    w0, w13 = early[:, :512], early[:, 512:]
    fourier = spectrum_table(sampled.shape[1], NF)
    leaf_index, *pair_index = [column(values) for values in (leaf_slot, *pairing)]
    points = on_chip(
        spectrum_body, (sampled.shape[0], fourier.shape[1]), LONG, "spectrum", sampled, fourier
    ).reshape(sampled.shape[0] // CHEB, CHEB * 2 * NF)
    points, w0, w13, late, leaf_index, pair_index = together((points, w0, w13, late, leaf_index, pair_index))

    states = lax.all_to_all(points, GROUP, split_axis=0, concat_axis=0, tiled=True)
    w13 = pieces_from(w13, "x")
    w1 = jnp.stack([piece[:, :128] for piece in w13])
    w3 = jnp.stack([piece[:, 128:] for piece in w13])
    w1 = jnp.stack(pieces_from(w1, "y"))
    w0 = jnp.stack(pieces_from(w0, "x"))
    late = doubled(late, 16, zh // 2)
    states = on_chip(select_body, states.shape, LONG, "leaves", leaf_index, states)
    states, w0, w1, w3, late = together((states, w0, w1, w3, late))

    far = flip(states, 1)
    w2 = doubled(late, 32, zl)
    joined, partial = near_step(0, "x", place, states, w0)
    far, w2 = together((far, w2))
    states = far_step(0, pair_index[0], far, joined, partial)

    far = flip(states, 4)
    states, w2 = together((states, w2))
    w2 = jnp.stack(pieces_from(w2, "x"))
    joined, partial = near_step(1, "y", place, states, w1)
    far, w2 = together((far, w2))
    states = far_step(1, pair_index[1], far, joined, partial)

    far = flip(states, 16)
    states, w3 = together((states, w3))
    w3 = jnp.stack(pieces_from(w3, "y"))
    joined, partial = near_step(2, "x", place, states, w2)
    far, w3 = together((far, w3))
    states = far_step(2, pair_index[2], far, joined, partial)

    far = flip(states, 64)
    joined, partial = near_step(3, "y", place, states, w3)
    return far_step(3, pair_index[3], far, joined, partial)


def solution(mesh):
    split = Mesh(mesh.devices.reshape(4, 2, 4, 4, 2), AXES)
    placed = (P(GROUP, TA), P(), P(None, GROUP, None), P(AXES), P(None, AXES))
    return jax.shard_map(on_device, mesh=split, in_specs=placed, out_specs=P(AXES, None), check_vma=False)
```

time: 372 us -> 204 us (0.55)
  waiting for transfers between devices: 297 us -> 101 us
  starting transfers between devices: 23.2 us -> 57.7 us
  Pallas kernels: 0 us -> 19.9 us
  matrix products: 19.9 us -> 5.65 us
  between operations: 13.3 us -> 0.45 us
  other arithmetic: 5.44 us -> 12.9 us
    all_gather x3 -> x0, waiting for transfers between devices: 226 us -> none  [whole_of(): nearer = lax.all_gather(x, axes[-1], axis=dim, tiled=True)]
    ppermute x4 -> x28, waiting for transfers between devices: 44.1 us -> 100 us  [the longest x15 62.1 us: shifted(): return lax.ppermute(value, axis, [(i, (i + k) % size) for i in range(size)])]
    ppermute x4 -> x28, starting transfers between devices: 9.64 us -> 46.6 us  [the longest x13 24.2 us: flip(): return lax.ppermute(value, AXES, [(i, i ^ mask) for i in range(size)])]
    all_to_all x2, waiting for transfers between devices: 26.7 us -> 0.91 us  [the longest x1 0.91 us: on_device(): lax.all_to_all(sampled, TA, split_axis=0, concat_axis=1, tiled=True)]
    pallas_call x0 -> x10, Pallas kernels: none -> 19.9 us  [the longest x4 14.5 us: near_step(): pl.pallas_call(functools.partial(near_body, layout), out_shape=[jax.Shape...]
    dot_general x5 -> x0, matrix products: 15.3 us -> none  [the longest x4 14.6 us: on_device(): jnp.dot(joined, every_level[layer_index], preferred_element_type=jnp.floa...]
    gather x5 -> x0, local copies, waits for them, and re-layouts: 5.83 us -> none  [the longest x4 4.67 us: on_device(): aligned = jnp.take(partner, pairing[layer_index], axis=0)]
    another operation x1 -> x8, other arithmetic: 4.77 us -> 7.89 us  [the longest x1 2.83 us: on_device(): w0 = jnp.stack(pieces_from(w0, 'x'))]
  transfers between devices with their start and end apart: 9 -> 30, of which waited for: 9 -> 17; matrix products, arithmetic and copies ran while one was open for 4% -> 9% of each run, Pallas kernels for 0% -> 8%
where the time goes in v1:
time: 204 us; the launch traced here: 203 us
  waiting for transfers between devices  101 us (50%)
  starting transfers between devices  57.7 us (28%)
  Pallas kernels  19.9 us (10%)
  other arithmetic  12.9 us (6%)
  matrix products  5.65 us (3%)
  local copies, waits for them, and re-layouts  5.1 us (2%)
    ppermute x15, waiting for transfers between devices, shifted(): return lax.ppermute(value, axis, [(i, (i + k) % size) for i in range(size)])  62.1 us
    ppermute x13, waiting for transfers between devices, flip(): return lax.ppermute(value, AXES, [(i, i ^ mask) for i in range(size)])  38 us
    ppermute x13, starting transfers between devices, flip(): return lax.ppermute(value, AXES, [(i, i ^ mask) for i in range(size)])  24.2 us
    ppermute x15, starting transfers between devices, shifted(): return lax.ppermute(value, axis, [(i, (i + k) % size) for i in range(size)])  22.4 us
    pallas_call x4, Pallas kernels, near_step(): pl.pallas_call(functools.partial(near_body, layout), out_shape=[jax.Shape...  14.5 us
    all_to_all x1, starting transfers between devices, on_device(): lax.all_to_all(points, GROUP, split_axis=0, concat_axis=0, tiled=True)  6.66 us
    dot_general x1, matrix products, on_device(): jnp.einsum('cb,kbt->kct', interp, traces.reshape(local_boxes, BOXT, local...  5.65 us
    pallas_call x6, Pallas kernels, on_chip(): pl.pallas_call(body, out_shape=jax.ShapeDtypeStruct(shape, BF16), in_spec...  5.4 us
  transfers between devices with their start and end apart: 30, of which 17 were waited for; matrix products, arithmetic and copies ran while one was open for 9% of the time, Pallas kernels for 8%

profile of v1, /device:TPU:2, one launch (start us, length us, event | category | flops | bytes accessed | tf_op | source)
XLA Modules:
  0.0 202.7 jit_solution(15710172230551388652)
XLA Ops:
  0.0 1.1 fusion.15
  1.2 3.4 %collective-permute-start = (bf16[64,1280]{1,0:T(8,128)(2,1)S(1)}, bf16[64,1280]{1,0:T(8,128)(2,1)S(1)}, u32[]{:S(2)}, u32[]{:S(2)}) collective-permute-start(bf16[64,1280]{1,0:T(8,128)(2,1)S(1)} %pad_maximum_fusion.11), channel_id=1, source_target_pairs={{0,8},{1,9},{2,10},{3,11},{4,12},{5,13},{6,14},{7,15},{8,0},{9,1},... | collective-permute-start | bytes 491528 | tf_op jit(solution)/shard_map/ppermute | solution.py:41
  4.6 5.6 %convolution_convert_fusion = bf16[2048,128,2]{1,2,0:T(2,128)(2,1)} fusion(bf16[2048,16,128]{2,1,0:T(8,128)(2,1)} %bitcast.73, bf16[2,16]{1,0:T(2,128)(2,1)S(1)} %copy-done), kind=kOutput, calls=%fused_computation.4 | convolution fusion | flops 17301504 | bytes 9437248 | tf_op jit(solution)/shard_map/cb,kbt->kct/dot_general | solution.py:169
  10.2 2.1 %collective-permute-done = bf16[64,1280]{1,0:T(8,128)(2,1)S(1)} collective-permute-done((bf16[64,1280]{1,0:T(8,128)(2,1)S(1)}, bf16[64,1280]{1,0:T(8,128)(2,1)S(1)}, u32[]{:S(2)}, u32[]{:S(2)}) %collective-permute-start) | collective-permute-done | bytes 163872 | tf_op jit(solution)/shard_map/ppermute | solution.py:41
  13.0 6.6 %collective-permute-start.1 = (bf16[128,768]{1,0:T(8,128)(2,1)S(1)}, bf16[128,768]{1,0:T(8,128)(2,1)S(1)}, u32[]{:S(2)}, u32[]{:S(2)}) collective-permute-start(bf16[128,768]{1,0:T(8,128)(2,1)S(1)} %fusion.1), channel_id=1, source_target_pairs={{0,16},{1,17},{2,18},{3,19},{4,20},{5,21},{6,22},{7,23},{8,24},{9,... | collective-permute-start | bytes 589832 | tf_op jit(solution)/shard_map/ppermute | solution.py:41
  20.0 4.5 %all-to-all-start = ((bf16[8,512,128]{2,1,0:T(8,128)(2,1)}), bf16[8,512,128]{2,1,0:T(8,128)(2,1)S(1)}, u32[]{:S(2)}, u32[]{:S(2)}) async-start(bf16[8,512,128]{2,1,0:T(8,128)(2,1)} %bitcast.8), calls=%async_computation | async-start | bytes 2097152 | tf_op jit(solution)/shard_map/all_to_all | solution.py:175
  24.5 2.8 %collective-permute-done.1 = bf16[128,768]{1,0:T(8,128)(2,1)S(1)} collective-permute-done((bf16[128,768]{1,0:T(8,128)(2,1)S(1)}, bf16[128,768]{1,0:T(8,128)(2,1)S(1)}, u32[]{:S(2)}, u32[]{:S(2)}) %collective-permute-start.1) | collective-permute-done | bytes 196640 | tf_op jit(solution)/shard_map/ppermute | solution.py:41
  29.2 9.2 %collective-permute-done.2 = bf16[256,768]{1,0:T(8,128)(2,1)} collective-permute-done((bf16[256,768]{1,0:T(8,128)(2,1)}, bf16[256,768]{1,0:T(8,128)(2,1)}, u32[]{:S(2)}, u32[]{:S(2)}) %collective-permute-start.2) | collective-permute-done | bytes 393248 | tf_op jit(solution)/shard_map/ppermute | solution.py:41
  38.3 1.1 broadcast_select_fusion
  39.5 0.9 all-to-all-done
  41.3 1.0 reshape.147
  42.3 1.5 collective-permute-start.6
  43.8 1.1 collective-permute-start.7
  44.9 2.2 %collective-permute-start.8 = (bf16[512,256]{1,0:T(8,128)(2,1)S(1)}, bf16[512,256]{1,0:T(8,128)(2,1)S(1)}, u32[]{:S(2)}, u32[]{:S(2)}) collective-permute-start(bf16[512,256]{1,0:T(8,128)(2,1)S(1)} %pad_maximum_fusion.9), channel_id=1, source_target_pairs={{0,192},{64,0},{128,64},{192,128},{1,193},{65,1},{129,65},{193,129... | collective-permute-start | bytes 786440 | tf_op jit(solution)/shard_map/ppermute | solution.py:46
  47.2 3.5 %collective-permute-start.4 = (bf16[512,512]{1,0:T(8,128)(2,1)S(1)}, bf16[512,512]{1,0:T(8,128)(2,1)}, u32[]{:S(2)}, u32[]{:S(2)}) collective-permute-start(bf16[512,512]{1,0:T(8,128)(2,1)S(1)} %fusion), channel_id=1, source_target_pairs={{0,128},{64,192},{128,0},{192,64},{1,129},{65,193},{129,1},{193,65... | collective-permute-start | bytes 1572872 | tf_op jit(solution)/shard_map/ppermute | solution.py:46
  50.8 6.7 %all-to-all-start.1 = ((bf16[32,8,1024]{2,1,0:T(8,128)(2,1)}), bf16[32,8,1024]{2,1,0:T(8,128)(2,1)S(1)}, u32[]{:S(2)}, u32[]{:S(2)}) async-start(bf16[32,8,1024]{2,1,0:T(8,128)(2,1)} %bitcast.17), calls=%async_computation.1 | async-start | bytes 1048576 | tf_op jit(solution)/shard_map/all_to_all | solution.py:185
  57.8 5.8 %collective-permute-start.12 = (bf16[128,512]{1,0:T(8,128)(2,1)S(1)}, bf16[128,512]{1,0:T(8,128)(2,1)S(1)}, u32[]{:S(2)}, u32[]{:S(2)}) collective-permute-start(bf16[128,512]{1,0:T(8,128)(2,1)S(1)} %copy-done.5), channel_id=1, source_target_pairs={{0,16},{1,17},{2,18},{3,19},{4,20},{5,21},{6,22},{7,23},{8,24},{9,... | collective-permute-start | bytes 393224 | tf_op jit(solution)/shard_map/ppermute | solution.py:41
  63.6 10.0 %collective-permute-done.8 = bf16[512,256]{1,0:T(8,128)(2,1)S(1)} collective-permute-done((bf16[512,256]{1,0:T(8,128)(2,1)S(1)}, bf16[512,256]{1,0:T(8,128)(2,1)S(1)}, u32[]{:S(2)}, u32[]{:S(2)}) %collective-permute-start.8) | collective-permute-done | bytes 262176 | tf_op jit(solution)/shard_map/ppermute | solution.py:46
  73.8 1.6 collective-permute-done.12
  75.5 3.2 %collective-permute-start.10 = (bf16[4,512,128]{2,1,0:T(8,128)(2,1)S(1)}, bf16[4,512,128]{2,1,0:T(8,128)(2,1)S(1)}, u32[]{:S(2)}, u32[]{:S(2)}) collective-permute-start(bf16[4,512,128]{2,1,0:T(8,128)(2,1)S(1)} %get-tuple-element.80), channel_id=1, source_target_pairs={{0,4},{2,6},{4,0},{6,2},{1,5},{3,7},{5,1},{7,3},{8,12},{10,14},{12... | collective-permute-start | bytes 1572872 | tf_op jit(solution)/shard_map/ppermute | solution.py:46
  78.7 1.1 collective-permute-start.11
  80.7 5.2 %collective-permute-done.5 = bf16[512,512]{1,0:T(8,128)(2,1)S(1)} collective-permute-done((bf16[512,512]{1,0:T(8,128)(2,1)S(1)}, bf16[512,512]{1,0:T(8,128)(2,1)S(1)}, u32[]{:S(2)}, u32[]{:S(2)}) %collective-permute-start.5) | collective-permute-done | bytes 524320 | tf_op jit(solution)/shard_map/ppermute | solution.py:46
  85.9 2.8 %pad_maximum_fusion.mine = bf16[4,512,512]{2,1,0:T(8,128)(2,1)} fusion(bf16[1,512,512]{2,1,0:T(8,128)(2,1)S(1)} %bitcast.78, bf16[1,512,512]{2,1,0:T(8,128)(2,1)} %bitcast.21, bf16[1,512,512]{2,1,0:T(8,128)(2,1)} %bitcast.20, bf16[1,512,512]{2,1,0:T(8,128)(2,1)S(1)} %bitcast.77), kind=kLoop, calls=%fused_computation | loop fusion | flops 3145728 | bytes 4194304 | tf_op jit(solution)/shard_map/stack | solution.py:190
  88.7 4.2 %collective-permute-done.9 = bf16[4,512,128]{2,1,0:T(8,128)(2,1)S(1)} collective-permute-done((bf16[4,512,128]{2,1,0:T(8,128)(2,1)S(1)}, bf16[4,512,128]{2,1,0:T(8,128)(2,1)S(1)}, u32[]{:S(2)}, u32[]{:S(2)}) %collective-permute-start.9) | collective-permute-done | bytes 524320 | tf_op jit(solution)/shard_map/ppermute | solution.py:46
  92.9 4.8 %collective-permute-done.11 = bf16[4,512,128]{2,1,0:T(8,128)(2,1)S(1)} collective-permute-done((bf16[4,512,128]{2,1,0:T(8,128)(2,1)S(1)}, bf16[4,512,128]{2,1,0:T(8,128)(2,1)S(1)}, u32[]{:S(2)}, u32[]{:S(2)}) %collective-permute-start.11) | collective-permute-done | bytes 524320 | tf_op jit(solution)/shard_map/ppermute | solution.py:46
  99.3 4.6 %collective-permute-start.14 = (bf16[256,512]{1,0:T(8,128)(2,1)S(1)}, bf16[256,512]{1,0:T(8,128)(2,1)}, u32[]{:S(2)}, u32[]{:S(2)}) collective-permute-start(bf16[256,512]{1,0:T(8,128)(2,1)S(1)} %pad_maximum_fusion.10), channel_id=1, source_target_pairs={{0,32},{1,33},{2,34},{3,35},{4,36},{5,37},{6,38},{7,39},{8,40},{9,... | collective-permute-start | bytes 786440 | tf_op jit(solution)/shard_map/ppermute | solution.py:41
  104.4 6.6 %collective-permute-done.14 = bf16[256,512]{1,0:T(8,128)(2,1)} collective-permute-done((bf16[256,512]{1,0:T(8,128)(2,1)S(1)}, bf16[256,512]{1,0:T(8,128)(2,1)}, u32[]{:S(2)}, u32[]{:S(2)}) %collective-permute-start.14) | collective-permute-done | bytes 262176 | tf_op jit(solution)/shard_map/ppermute | solution.py:41
  111.0 1.0 broadcast_select_fusion.3
  112.8 3.5 %near0.1 = (bf16[2048,1024]{1,0:T(8,128)(2,1)S(1)}, f32[256,1024]{1,0:T(8,128)S(1)}) custom-call(s32[3]{0:T(128)S(1)} %pad_add_fusion.place, bf16[256,1024]{1,0:T(8,128)(2,1)S(1)} %leaves.1.own, bf16[4,512,512]{2,1,0:T(8,128)(2,1)} %pad_maximum_fusion.mine, bf16[4,512,512]{2,1,0:T(8,128)(2,1)} %collective-permute-done.15.other), custom_call_target="tpu_custom_call" | custom-call | flops 536870912 | bytes 6291456 | tf_op jit(solution)/shard_map/near0/pallas_call | solution.py:134
  116.3 0.9 far0.1.own
  117.2 1.6 collective-permute-start.17
  119.6 2.5 %collective-permute-start.19 = (bf16[512,512]{1,0:T(8,128)(2,1)}, bf16[512,512]{1,0:T(8,128)(2,1)}, u32[]{:S(2)}, u32[]{:S(2)}) collective-permute-start(bf16[512,512]{1,0:T(8,128)(2,1)} %pad_maximum_fusion.7), channel_id=1, source_target_pairs={{0,192},{64,0},{128,64},{192,128},{1,193},{65,1},{129,65},{193,129... | collective-permute-start | bytes 1572872 | tf_op jit(solution)/shard_map/ppermute | solution.py:46
  122.1 1.8 collective-permute-start.16
  124.1 3.8 %near1.1 = (bf16[2048,1024]{1,0:T(8,128)(2,1)S(1)}, f32[256,1024]{1,0:T(8,128)S(1)}) custom-call(s32[3]{0:T(128)S(1)} %pad_add_fusion.place, bf16[256,1024]{1,0:T(8,128)(2,1)S(1)} %far0.1.own, bf16[4,4,512,128]{3,2,1,0:T(8,128)(2,1)} %copy-done.2, bf16[4,4,512,128]{3,2,1,0:T(8,128)(2,1)} %collective-permute-done.20.other), custom_call_target="tpu_custom_call" | custom-call | flops 536870912 | bytes 6291456 | tf_op jit(solution)/shard_map/near1/pallas_call | solution.py:134
  127.9 4.5 %collective-permute-done.17 = bf16[512,512]{1,0:T(8,128)(2,1)} collective-permute-done((bf16[512,512]{1,0:T(8,128)(2,1)}, bf16[512,512]{1,0:T(8,128)(2,1)}, u32[]{:S(2)}, u32[]{:S(2)}) %collective-permute-start.17) | collective-permute-done | bytes 524320 | tf_op jit(solution)/shard_map/ppermute | solution.py:46
  132.4 3.0 %collective-permute-done.18 = bf16[512,512]{1,0:T(8,128)(2,1)} collective-permute-done((bf16[512,512]{1,0:T(8,128)(2,1)}, bf16[512,512]{1,0:T(8,128)(2,1)}, u32[]{:S(2)}, u32[]{:S(2)}) %collective-permute-start.18) | collective-permute-done | bytes 524320 | tf_op jit(solution)/shard_map/ppermute | solution.py:46
  135.4 9.2 %collective-permute-done.19 = bf16[512,512]{1,0:T(8,128)(2,1)} collective-permute-done((bf16[512,512]{1,0:T(8,128)(2,1)}, bf16[512,512]{1,0:T(8,128)(2,1)}, u32[]{:S(2)}, u32[]{:S(2)}) %collective-permute-start.19) | collective-permute-done | bytes 524320 | tf_op jit(solution)/shard_map/ppermute | solution.py:46
  144.6 1.8 pad_maximum_fusion.2.mine
  147.9 1.2 collective-permute-start.22
  149.1 2.9 %collective-permute-start.23 = (bf16[4,512,128]{2,1,0:T(8,128)(2,1)S(1)}, bf16[4,512,128]{2,1,0:T(8,128)(2,1)S(1)}, u32[]{:S(2)}, u32[]{:S(2)}) collective-permute-start(bf16[4,512,128]{2,1,0:T(8,128)(2,1)S(1)} %copy-done.4), channel_id=1, source_target_pairs={{0,4},{2,6},{4,0},{6,2},{1,5},{3,7},{5,1},{7,3},{8,12},{10,14},{12... | collective-permute-start | bytes 1572872 | tf_op jit(solution)/shard_map/ppermute | solution.py:46
  153.1 10.0 %collective-permute-done.22 = bf16[4,512,128]{2,1,0:T(8,128)(2,1)S(1)} collective-permute-done((bf16[4,512,128]{2,1,0:T(8,128)(2,1)S(1)}, bf16[4,512,128]{2,1,0:T(8,128)(2,1)S(1)}, u32[]{:S(2)}, u32[]{:S(2)}) %collective-permute-start.22) | collective-permute-done | bytes 524320 | tf_op jit(solution)/shard_map/ppermute | solution.py:46
  163.1 11.2 %collective-permute-done.23 = bf16[4,512,128]{2,1,0:T(8,128)(2,1)S(1)} collective-permute-done((bf16[4,512,128]{2,1,0:T(8,128)(2,1)S(1)}, bf16[4,512,128]{2,1,0:T(8,128)(2,1)S(1)}, u32[]{:S(2)}, u32[]{:S(2)}) %collective-permute-start.23) | collective-permute-done | bytes 524320 | tf_op jit(solution)/shard_map/ppermute | solution.py:46
  174.3 1.6 pad_maximum_fusion.3.mine
  175.9 6.1 %collective-permute-done.21.far = bf16[256,1024]{1,0:T(8,128)(2,1)S(1)} collective-permute-done((bf16[256,1024]{1,0:T(8,128)(2,1)S(1)}, bf16[256,1024]{1,0:T(8,128)(2,1)S(1)}, u32[]{:S(2)}, u32[]{:S(2)}) %collective-permute-start.21) | collective-permute-done | bytes 524320 | tf_op jit(solution)/shard_map/ppermute | solution.py:41
  182.2 3.5 %near2.1 = (bf16[2048,1024]{1,0:T(8,128)(2,1)S(1)}, f32[256,1024]{1,0:T(8,128)S(1)}) custom-call(s32[3]{0:T(128)S(1)} %pad_add_fusion.place, bf16[256,1024]{1,0:T(8,128)(2,1)S(1)} %far1.1.own, bf16[4,512,512]{2,1,0:T(8,128)(2,1)} %copy-done.3, bf16[4,512,512]{2,1,0:T(8,128)(2,1)} %collective-permute-done.25.other), custom_call_target="tpu_custom_call" | custom-call | flops 536870912 | bytes 6291456 | tf_op jit(solution)/shard_map/near2/pallas_call | solution.py:134
  187.6 3.8 %near3.1 = (bf16[2048,1024]{1,0:T(8,128)(2,1)S(1)}, f32[256,1024]{1,0:T(8,128)S(1)}) custom-call(s32[3]{0:T(128)S(1)} %pad_add_fusion.place, bf16[256,1024]{1,0:T(8,128)(2,1)S(1)} %far2.1.own, bf16[4,4,512,128]{3,2,1,0:T(8,128)(2,1)} %pad_maximum_fusion.3.mine, bf16[4,4,512,128]{3,2,1,0:T(8,128)(2,1)} %collective-permute-done.27.other), custom_call_target="tpu_custom_call" | custom-call | flops 536870912 | bytes 6291456 | tf_op jit(solution)/shard_map/near3/pallas_call | solution.py:134
  191.4 9.6 %collective-permute-done.26.far = bf16[256,1024]{1,0:T(8,128)(2,1)S(1)} collective-permute-done((bf16[256,1024]{1,0:T(8,128)(2,1)S(1)}, bf16[256,1024]{1,0:T(8,128)(2,1)S(1)}, u32[]{:S(2)}, u32[]{:S(2)}) %collective-permute-start.26) | collective-permute-done | bytes 524320 | tf_op jit(solution)/shard_map/ppermute | solution.py:41
  201.0 1.7 far3.1
  (87 shorter events, 14.0 us)
Async XLA Ops:
  0.0 4.6 %copy-start = (bf16[2,16]{1,0:T(2,128)(2,1)S(1)}, bf16[2,16]{1,0:T(2,128)(2,1)}, u32[]{:S(2)}) copy-start(bf16[2,16]{1,0:T(2,128)(2,1)} %param.6) | copy-start | bytes 196
  1.2 11.1 %collective-permute-start = (bf16[64,1280]{1,0:T(8,128)(2,1)S(1)}, bf16[64,1280]{1,0:T(8,128)(2,1)S(1)}, u32[]{:S(2)}, u32[]{:S(2)}) collective-permute-start(bf16[64,1280]{1,0:T(8,128)(2,1)S(1)} %pad_maximum_fusion.11), channel_id=1, source_target_pairs={{0,8},{1,9},{2,10},{3,11},{4,12},{5,13},{6,14},{7,15},{8,0},{9,1},... | collective-permute-start | bytes 491528 | tf_op jit(solution)/shard_map/ppermute | solution.py:41
  13.0 14.2 %collective-permute-start.1 = (bf16[128,768]{1,0:T(8,128)(2,1)S(1)}, bf16[128,768]{1,0:T(8,128)(2,1)S(1)}, u32[]{:S(2)}, u32[]{:S(2)}) collective-permute-start(bf16[128,768]{1,0:T(8,128)(2,1)S(1)} %fusion.1), channel_id=1, source_target_pairs={{0,16},{1,17},{2,18},{3,19},{4,20},{5,21},{6,22},{7,23},{8,24},{9,... | collective-permute-start | bytes 589832 | tf_op jit(solution)/shard_map/ppermute | solution.py:41
  20.0 20.4 %all-to-all-start = ((bf16[8,512,128]{2,1,0:T(8,128)(2,1)}), bf16[8,512,128]{2,1,0:T(8,128)(2,1)S(1)}, u32[]{:S(2)}, u32[]{:S(2)}) async-start(bf16[8,512,128]{2,1,0:T(8,128)(2,1)} %bitcast.8), calls=%async_computation | async-start | bytes 2097152 | tf_op jit(solution)/shard_map/all_to_all | solution.py:175
  27.3 1.3 copy-start.10
  28.1 10.2 %collective-permute-start.2 = (bf16[256,768]{1,0:T(8,128)(2,1)}, bf16[256,768]{1,0:T(8,128)(2,1)}, u32[]{:S(2)}, u32[]{:S(2)}) collective-permute-start(bf16[256,768]{1,0:T(8,128)(2,1)} %pad_maximum_fusion.8), channel_id=1, source_target_pairs={{0,32},{1,33},{2,34},{3,35},{4,36},{5,37},{6,38},{7,39},{8,40},{9,... | collective-permute-start | bytes 1179656 | tf_op jit(solution)/shard_map/ppermute | solution.py:41
  40.6 10.1 %copy-start.11 = (s32[256]{0:T(256)S(1)}, s32[256]{0:T(256)}, u32[]{:S(2)}) copy-start(s32[256]{0:T(256)} %param.8) | copy-start | bytes 3076
  41.3 16.5 %copy-start.5 = (bf16[128,512]{1,0:T(8,128)(2,1)S(1)}, bf16[128,512]{1,0:T(8,128)(2,1)}, u32[]{:S(2)}) copy-start(bf16[128,512]{1,0:T(8,128)(2,1)} %pad_maximum_fusion.12) | copy-start | bytes 393220
  42.3 15.2 %collective-permute-start.6 = (bf16[512,256]{1,0:T(8,128)(2,1)S(1)}, bf16[512,256]{1,0:T(8,128)(2,1)S(1)}, u32[]{:S(2)}, u32[]{:S(2)}) collective-permute-start(bf16[512,256]{1,0:T(8,128)(2,1)S(1)} %pad_maximum_fusion.9), channel_id=1, source_target_pairs={{0,64},{64,128},{128,192},{192,0},{1,65},{65,129},{129,193},{193,1... | collective-permute-start | bytes 786440 | tf_op jit(solution)/shard_map/ppermute | solution.py:46
  43.8 14.0 %collective-permute-start.7 = (bf16[512,256]{1,0:T(8,128)(2,1)S(1)}, bf16[512,256]{1,0:T(8,128)(2,1)S(1)}, u32[]{:S(2)}, u32[]{:S(2)}) collective-permute-start(bf16[512,256]{1,0:T(8,128)(2,1)S(1)} %pad_maximum_fusion.9), channel_id=1, source_target_pairs={{0,128},{64,192},{128,0},{192,64},{1,129},{65,193},{129,1},{193,65... | collective-permute-start | bytes 786440 | tf_op jit(solution)/shard_map/ppermute | solution.py:46
  44.9 28.7 %collective-permute-start.8 = (bf16[512,256]{1,0:T(8,128)(2,1)S(1)}, bf16[512,256]{1,0:T(8,128)(2,1)S(1)}, u32[]{:S(2)}, u32[]{:S(2)}) collective-permute-start(bf16[512,256]{1,0:T(8,128)(2,1)S(1)} %pad_maximum_fusion.9), channel_id=1, source_target_pairs={{0,192},{64,0},{128,64},{192,128},{1,193},{65,1},{129,65},{193,129... | collective-permute-start | bytes 786440 | tf_op jit(solution)/shard_map/ppermute | solution.py:46
  47.1 31.6 %collective-permute-start.3 = (bf16[512,512]{1,0:T(8,128)(2,1)S(1)}, bf16[512,512]{1,0:T(8,128)(2,1)}, u32[]{:S(2)}, u32[]{:S(2)}) collective-permute-start(bf16[512,512]{1,0:T(8,128)(2,1)S(1)} %fusion), channel_id=1, source_target_pairs={{0,64},{64,128},{128,192},{192,0},{1,65},{65,129},{129,193},{193,1... | collective-permute-start | bytes 1572872 | tf_op jit(solution)/shard_map/ppermute | solution.py:46
  47.2 33.5 %collective-permute-start.4 = (bf16[512,512]{1,0:T(8,128)(2,1)S(1)}, bf16[512,512]{1,0:T(8,128)(2,1)}, u32[]{:S(2)}, u32[]{:S(2)}) collective-permute-start(bf16[512,512]{1,0:T(8,128)(2,1)S(1)} %fusion), channel_id=1, source_target_pairs={{0,128},{64,192},{128,0},{192,64},{1,129},{65,193},{129,1},{193,65... | collective-permute-start | bytes 1572872 | tf_op jit(solution)/shard_map/ppermute | solution.py:46
  50.8 47.2 %all-to-all-start.1 = ((bf16[32,8,1024]{2,1,0:T(8,128)(2,1)}), bf16[32,8,1024]{2,1,0:T(8,128)(2,1)S(1)}, u32[]{:S(2)}, u32[]{:S(2)}) async-start(bf16[32,8,1024]{2,1,0:T(8,128)(2,1)} %bitcast.17), calls=%async_computation.1 | async-start | bytes 1048576 | tf_op jit(solution)/shard_map/all_to_all | solution.py:185
  57.5 28.4 %collective-permute-start.5 = (bf16[512,512]{1,0:T(8,128)(2,1)S(1)}, bf16[512,512]{1,0:T(8,128)(2,1)S(1)}, u32[]{:S(2)}, u32[]{:S(2)}) collective-permute-start(bf16[512,512]{1,0:T(8,128)(2,1)S(1)} %fusion), channel_id=1, source_target_pairs={{0,192},{64,0},{128,64},{192,128},{1,193},{65,1},{129,65},{193,129... | collective-permute-start | bytes 1572872 | tf_op jit(solution)/shard_map/ppermute | solution.py:46
  57.8 17.7 %collective-permute-start.12 = (bf16[128,512]{1,0:T(8,128)(2,1)S(1)}, bf16[128,512]{1,0:T(8,128)(2,1)S(1)}, u32[]{:S(2)}, u32[]{:S(2)}) collective-permute-start(bf16[128,512]{1,0:T(8,128)(2,1)S(1)} %copy-done.5), channel_id=1, source_target_pairs={{0,16},{1,17},{2,18},{3,19},{4,20},{5,21},{6,22},{7,23},{8,24},{9,... | collective-permute-start | bytes 393224 | tf_op jit(solution)/shard_map/ppermute | solution.py:41
  73.8 19.2 %collective-permute-start.9 = (bf16[4,512,128]{2,1,0:T(8,128)(2,1)S(1)}, bf16[4,512,128]{2,1,0:T(8,128)(2,1)S(1)}, u32[]{:S(2)}, u32[]{:S(2)}) collective-permute-start(bf16[4,512,128]{2,1,0:T(8,128)(2,1)S(1)} %get-tuple-element.80), channel_id=1, source_target_pairs={{0,2},{2,4},{4,6},{6,0},{1,3},{3,5},{5,7},{7,1},{8,10},{10,12},{12... | collective-permute-start | bytes 1572872 | tf_op jit(solution)/shard_map/ppermute | solution.py:46
  75.5 17.4 %collective-permute-start.10 = (bf16[4,512,128]{2,1,0:T(8,128)(2,1)S(1)}, bf16[4,512,128]{2,1,0:T(8,128)(2,1)S(1)}, u32[]{:S(2)}, u32[]{:S(2)}) collective-permute-start(bf16[4,512,128]{2,1,0:T(8,128)(2,1)S(1)} %get-tuple-element.80), channel_id=1, source_target_pairs={{0,4},{2,6},{4,0},{6,2},{1,5},{3,7},{5,1},{7,3},{8,12},{10,14},{12... | collective-permute-start | bytes 1572872 | tf_op jit(solution)/shard_map/ppermute | solution.py:46
  78.7 19.0 %collective-permute-start.11 = (bf16[4,512,128]{2,1,0:T(8,128)(2,1)S(1)}, bf16[4,512,128]{2,1,0:T(8,128)(2,1)S(1)}, u32[]{:S(2)}, u32[]{:S(2)}) collective-permute-start(bf16[4,512,128]{2,1,0:T(8,128)(2,1)S(1)} %get-tuple-element.80), channel_id=1, source_target_pairs={{0,6},{2,0},{4,2},{6,4},{1,7},{3,1},{5,3},{7,5},{8,14},{10,8},{12,... | collective-permute-start | bytes 1572872 | tf_op jit(solution)/shard_map/ppermute | solution.py:46
  97.9 1.4 copy-start.2
  98.0 6.2 %copy-start.9 = (s32[256,1]{0,1:T(1,128)S(1)}, s32[256,1]{0,1:T(1,128)}, u32[]{:S(2)}) copy-start(s32[256,1]{0,1:T(1,128)} %get-tuple-element.46) | copy-start | bytes 3076
  98.3 14.5 %collective-permute-start.15 = (bf16[4,512,512]{2,1,0:T(8,128)(2,1)}, bf16[4,512,512]{2,1,0:T(8,128)(2,1)}, u32[]{:S(2)}, u32[]{:S(2)}) collective-permute-start(bf16[4,512,512]{2,1,0:T(8,128)(2,1)} %pad_maximum_fusion.mine), channel_id=1, source_target_pairs={{0,1},{1,0},{2,3},{3,2},{4,5},{5,4},{6,7},{7,6},{8,9},{9,8},{10,11... | collective-permute-start | bytes 6291464 | tf_op jit(solution)/shard_map/ppermute | solution.py:41
  99.3 24.8 %collective-permute-start.20 = (bf16[4,4,512,128]{3,2,1,0:T(8,128)(2,1)S(1)}, bf16[4,4,512,128]{3,2,1,0:T(8,128)(2,1)}, u32[]{:S(2)}, u32[]{:S(2)}) collective-permute-start(bf16[4,4,512,128]{3,2,1,0:T(8,128)(2,1)S(1)} %pad_maximum_fusion.1.mine), channel_id=1, source_target_pairs={{0,1},{1,0},{2,3},{3,2},{4,5},{5,4},{6,7},{7,6},{8,9},{9,8},{10,11... | collective-permute-start | bytes 6291464 | tf_op jit(solution)/shard_map/ppermute | solution.py:41
  99.3 11.7 %collective-permute-start.14 = (bf16[256,512]{1,0:T(8,128)(2,1)S(1)}, bf16[256,512]{1,0:T(8,128)(2,1)}, u32[]{:S(2)}, u32[]{:S(2)}) collective-permute-start(bf16[256,512]{1,0:T(8,128)(2,1)S(1)} %pad_maximum_fusion.10), channel_id=1, source_target_pairs={{0,32},{1,33},{2,34},{3,35},{4,36},{5,37},{6,38},{7,39},{8,40},{9,... | collective-permute-start | bytes 786440 | tf_op jit(solution)/shard_map/ppermute | solution.py:41
  103.9 8.9 %collective-permute-start.13 = (bf16[256,1024]{1,0:T(8,128)(2,1)S(1)}, bf16[256,1024]{1,0:T(8,128)(2,1)S(1)}, u32[]{:S(2)}, u32[]{:S(2)}) collective-permute-start(bf16[256,1024]{1,0:T(8,128)(2,1)S(1)} %leaves.1.own), channel_id=1, source_target_pairs={{0,1},{1,0},{2,3},{3,2},{4,5},{5,4},{6,7},{7,6},{8,9},{9,8},{10,11... | collective-permute-start | bytes 1572872 | tf_op jit(solution)/shard_map/ppermute | solution.py:41
  116.3 7.7 %copy-start.8 = (s32[256,1]{0,1:T(1,128)S(1)}, s32[256,1]{0,1:T(1,128)}, u32[]{:S(2)}) copy-start(s32[256,1]{0,1:T(1,128)} %get-tuple-element.45) | copy-start | bytes 3076
  117.2 15.2 %collective-permute-start.17 = (bf16[512,512]{1,0:T(8,128)(2,1)}, bf16[512,512]{1,0:T(8,128)(2,1)}, u32[]{:S(2)}, u32[]{:S(2)}) collective-permute-start(bf16[512,512]{1,0:T(8,128)(2,1)} %pad_maximum_fusion.7), channel_id=1, source_target_pairs={{0,64},{64,128},{128,192},{192,0},{1,65},{65,129},{129,193},{193,1... | collective-permute-start | bytes 1572872 | tf_op jit(solution)/shard_map/ppermute | solution.py:46
  118.8 16.7 %collective-permute-start.18 = (bf16[512,512]{1,0:T(8,128)(2,1)}, bf16[512,512]{1,0:T(8,128)(2,1)}, u32[]{:S(2)}, u32[]{:S(2)}) collective-permute-start(bf16[512,512]{1,0:T(8,128)(2,1)} %pad_maximum_fusion.7), channel_id=1, source_target_pairs={{0,128},{64,192},{128,0},{192,64},{1,129},{65,193},{129,1},{193,65... | collective-permute-start | bytes 1572872 | tf_op jit(solution)/shard_map/ppermute | solution.py:46
  119.6 25.0 %collective-permute-start.19 = (bf16[512,512]{1,0:T(8,128)(2,1)}, bf16[512,512]{1,0:T(8,128)(2,1)}, u32[]{:S(2)}, u32[]{:S(2)}) collective-permute-start(bf16[512,512]{1,0:T(8,128)(2,1)} %pad_maximum_fusion.7), channel_id=1, source_target_pairs={{0,192},{64,0},{128,64},{192,128},{1,193},{65,1},{129,65},{193,129... | collective-permute-start | bytes 1572872 | tf_op jit(solution)/shard_map/ppermute | solution.py:46
  122.1 24.3 %collective-permute-start.16 = (bf16[256,1024]{1,0:T(8,128)(2,1)S(1)}, bf16[256,1024]{1,0:T(8,128)(2,1)S(1)}, u32[]{:S(2)}, u32[]{:S(2)}) collective-permute-start(bf16[256,1024]{1,0:T(8,128)(2,1)S(1)} %far0.1.own), channel_id=1, source_target_pairs={{0,4},{1,5},{2,6},{3,7},{4,0},{5,1},{6,2},{7,3},{8,12},{9,13},{10,... | collective-permute-start | bytes 1572872 | tf_op jit(solution)/shard_map/ppermute | solution.py:41
  146.4 5.9 %copy-start.3 = (bf16[4,512,512]{2,1,0:T(8,128)(2,1)}, bf16[4,512,512]{2,1,0:T(8,128)(2,1)S(1)}, u32[]{:S(2)}) copy-start(bf16[4,512,512]{2,1,0:T(8,128)(2,1)S(1)} %pad_maximum_fusion.2.mine) | copy-start | bytes 6291460
  146.4 1.4 copy-start.4
  147.9 15.2 %collective-permute-start.22 = (bf16[4,512,128]{2,1,0:T(8,128)(2,1)S(1)}, bf16[4,512,128]{2,1,0:T(8,128)(2,1)S(1)}, u32[]{:S(2)}, u32[]{:S(2)}) collective-permute-start(bf16[4,512,128]{2,1,0:T(8,128)(2,1)S(1)} %copy-done.4), channel_id=1, source_target_pairs={{0,2},{2,4},{4,6},{6,0},{1,3},{3,5},{5,7},{7,1},{8,10},{10,12},{12... | collective-permute-start | bytes 1572872 | tf_op jit(solution)/shard_map/ppermute | solution.py:46
  149.1 25.2 %collective-permute-start.23 = (bf16[4,512,128]{2,1,0:T(8,128)(2,1)S(1)}, bf16[4,512,128]{2,1,0:T(8,128)(2,1)S(1)}, u32[]{:S(2)}, u32[]{:S(2)}) collective-permute-start(bf16[4,512,128]{2,1,0:T(8,128)(2,1)S(1)} %copy-done.4), channel_id=1, source_target_pairs={{0,4},{2,6},{4,0},{6,2},{1,5},{3,7},{5,1},{7,3},{8,12},{10,14},{12... | collective-permute-start | bytes 1572872 | tf_op jit(solution)/shard_map/ppermute | solution.py:46
  152.0 22.3 %collective-permute-start.24 = (bf16[4,512,128]{2,1,0:T(8,128)(2,1)S(1)}, bf16[4,512,128]{2,1,0:T(8,128)(2,1)S(1)}, u32[]{:S(2)}, u32[]{:S(2)}) collective-permute-start(bf16[4,512,128]{2,1,0:T(8,128)(2,1)S(1)} %copy-done.4), channel_id=1, source_target_pairs={{0,6},{2,0},{4,2},{6,4},{1,7},{3,1},{5,3},{7,5},{8,14},{10,8},{12,... | collective-permute-start | bytes 1572872 | tf_op jit(solution)/shard_map/ppermute | solution.py:46
  152.4 29.8 %collective-permute-start.25 = (bf16[4,512,512]{2,1,0:T(8,128)(2,1)S(1)}, bf16[4,512,512]{2,1,0:T(8,128)(2,1)}, u32[]{:S(2)}, u32[]{:S(2)}) collective-permute-start(bf16[4,512,512]{2,1,0:T(8,128)(2,1)S(1)} %pad_maximum_fusion.2.mine), channel_id=1, source_target_pairs={{0,1},{1,0},{2,3},{3,2},{4,5},{5,4},{6,7},{7,6},{8,9},{9,8},{10,11... | collective-permute-start | bytes 6291464 | tf_op jit(solution)/shard_map/ppermute | solution.py:41
  152.4 29.6 %collective-permute-start.21 = (bf16[256,1024]{1,0:T(8,128)(2,1)S(1)}, bf16[256,1024]{1,0:T(8,128)(2,1)S(1)}, u32[]{:S(2)}, u32[]{:S(2)}) collective-permute-start(bf16[256,1024]{1,0:T(8,128)(2,1)S(1)} %far1.1.own), channel_id=1, source_target_pairs={{0,16},{1,17},{2,18},{3,19},{4,20},{5,21},{6,22},{7,23},{8,24},{9,... | collective-permute-start | bytes 1572872 | tf_op jit(solution)/shard_map/ppermute | solution.py:41
  174.3 7.7 %copy-start.7 = (s32[256,1]{0,1:T(1,128)S(1)}, s32[256,1]{0,1:T(1,128)}, u32[]{:S(2)}) copy-start(s32[256,1]{0,1:T(1,128)} %get-tuple-element.44) | copy-start | bytes 3076
  182.0 5.6 %collective-permute-start.27 = (bf16[4,4,512,128]{3,2,1,0:T(8,128)(2,1)}, bf16[4,4,512,128]{3,2,1,0:T(8,128)(2,1)}, u32[]{:S(2)}, u32[]{:S(2)}) collective-permute-start(bf16[4,4,512,128]{3,2,1,0:T(8,128)(2,1)} %pad_maximum_fusion.3.mine), channel_id=1, source_target_pairs={{0,1},{1,0},{2,3},{3,2},{4,5},{5,4},{6,7},{7,6},{8,9},{9,8},{10,11... | collective-permute-start | bytes 6291464 | tf_op jit(solution)/shard_map/ppermute | solution.py:41
  185.6 1.8 copy-start.6
  186.6 14.4 %collective-permute-start.26 = (bf16[256,1024]{1,0:T(8,128)(2,1)S(1)}, bf16[256,1024]{1,0:T(8,128)(2,1)S(1)}, u32[]{:S(2)}, u32[]{:S(2)}) collective-permute-start(bf16[256,1024]{1,0:T(8,128)(2,1)S(1)} %far2.1.own), channel_id=1, source_target_pairs={{0,64},{1,65},{2,66},{3,67},{4,68},{5,69},{6,70},{7,71},{8,72},{9,... | collective-permute-start | bytes 1572872 | tf_op jit(solution)/shard_map/ppermute | solution.py:41
  201.0 1.7 copy-start.1

commit v2 on v1

--- a/solution.py
+++ b/solution.py
@@ -66,26 +66,38 @@
     return jnp.dot(hot, values, preferred_element_type=F32).astype(BF16)
 
 
-def plan_copies(layout, place, mine, other, weights):
+def plan_copies(level, place, mine, other, weights):
     x, y, c = place[0], place[1], place[2]
     copies = []
-    for half, source in enumerate((mine, other)):
+    for half, sources in enumerate((mine, other)):
         column = jnp.where(c == half, 0, 512)
+        for source in sources:
+            if len(source.shape) == 5:
+                cols = pl.ds(pl.multiple_of(column, 512), 512)
+                for n in range(4):
+                    for z in range(8):
+                        row = lax.rem(x + (4 - n), 4) * 512 + (z % 2 * 4 + z // 2) * 64
+                        rows = pl.ds(pl.multiple_of(row, 64), 64)
+                        copies.append((source.at[z, n, level - 2], weights.at[rows, cols]))
         for k in range(4):
             rows = pl.ds(pl.multiple_of(lax.rem(x + (4 - k), 4) * 512, 512), 512)
-            if layout == "x":
-                cols = pl.ds(pl.multiple_of(column, 512), 512)
-                copies.append((source.at[k], weights.at[rows, cols]))
-            else:
-                for j in range(4):
-                    cols = pl.ds(pl.multiple_of(column + lax.rem(y + (4 - j), 4) * 128, 128), 128)
-                    copies.append((source.at[j, k], weights.at[rows, cols]))
+            for n, source in enumerate(sources):
+                if len(source.shape) == 3:
+                    width = source.shape[2]
+                    cols = pl.ds(pl.multiple_of(column + n * width, 256), width)
+                    copies.append((source.at[k], weights.at[rows, cols]))
+                elif len(source.shape) == 4:
+                    for j in range(4):
+                        cols = pl.ds(pl.multiple_of(column + lax.rem(y + (4 - j), 4) * 128, 128), 128)
+                        copies.append((source.at[j, k], weights.at[rows, cols]))
     return copies
 
 
-def near_body(layout, place, own, mine, other, weights, partial, sems):
+def near_body(level, count, place, own, *refs):
+    mine, other = refs[:count], refs[count : 2 * count]
+    weights, partial, sems = refs[2 * count :]
     started = []
-    for n, (source, target) in enumerate(plan_copies(layout, place, mine, other, weights)):
+    for n, (source, target) in enumerate(plan_copies(level, place, mine, other, weights)):
         copy = pltpu.make_async_copy(source, target, sems.at[n])
         copy.start()
         started.append(copy)
@@ -128,19 +140,19 @@
     )(*operands)
 
 
-def near_step(level, layout, place, own, mine):
-    other = flip(mine, 1)
-    mine, other = [pltpu.with_memory_space_constraint(piece, pltpu.HBM) for piece in (mine, other)]
+def near_step(level, place, own, mine, other):
+    pieces = [pltpu.with_memory_space_constraint(piece, pltpu.HBM) for piece in (*mine, *other)]
+    copies = sum({5: 32, 3: 4, 4: 16}[piece.ndim] for piece in pieces)
     return pl.pallas_call(
-        functools.partial(near_body, layout),
+        functools.partial(near_body, level, len(mine)),
         out_shape=[jax.ShapeDtypeStruct((2048, 1024), BF16), jax.ShapeDtypeStruct(own.shape, F32)],
-        in_specs=[pl.BlockSpec(memory_space=pltpu.SMEM), VMEM, HBM, HBM],
+        in_specs=[pl.BlockSpec(memory_space=pltpu.SMEM), VMEM] + [HBM] * len(pieces),
         out_specs=[VMEM, VMEM],
-        scratch_shapes=[pltpu.SemaphoreType.DMA((8 if layout == "x" else 32,))],
+        scratch_shapes=[pltpu.SemaphoreType.DMA((copies,))],
         compiler_params=pltpu.CompilerParams(vmem_limit_bytes=VMEM_LIMIT),
         cost_estimate=pl.CostEstimate(flops=256 * 2048 * 1024, bytes_accessed=6 << 20, transcendentals=0),
         name="near" + str(level),
-    )(place, own, mine, other)
+    )(place, own, *pieces)
 
 
 def far_step(level, index, far, joined, partial):
@@ -162,59 +174,46 @@
     def eighth(level):
         return lax.dynamic_slice_in_dim(translations[level], c * 512 + y * 128, 128, 1)
 
-    rows = doubled(jnp.concatenate([half(0), eighth(1), eighth(3), half(2)], axis=1), 8, zh % 2)
-    early, late = rows[:, :768], rows[:, 768:]
+    late = jnp.stack(pieces_from(jnp.stack([half(2), half(3)]), "x"))
+    rows = doubled(jnp.concatenate([half(0), eighth(1)], axis=1), 8, zh % 2)
     local_boxes = traces.shape[0] // BOXT
     local_cols = traces.shape[1]
     sampled = jnp.einsum(
         "cb,kbt->kct", interp, traces.reshape(local_boxes, BOXT, local_cols), preferred_element_type=F32
     )
     sampled = sampled.astype(BF16).reshape(local_boxes * CHEB, local_cols)
-    sampled, early, late = together((sampled, early, late))
+    sampled, rows = together((sampled, rows))
 
     sampled = lax.all_to_all(sampled, TA, split_axis=0, concat_axis=1, tiled=True)
-    early = doubled(doubled(early, 16, zh // 2), 32, zl)
-    w0, w13 = early[:, :512], early[:, 512:]
+    rows = doubled(doubled(rows, 16, zh // 2), 32, zl)
+    w0, w1 = rows[:, :512], rows[:, 512:]
     fourier = spectrum_table(sampled.shape[1], NF)
     leaf_index, *pair_index = [column(values) for values in (leaf_slot, *pairing)]
     points = on_chip(
         spectrum_body, (sampled.shape[0], fourier.shape[1]), LONG, "spectrum", sampled, fourier
     ).reshape(sampled.shape[0] // CHEB, CHEB * 2 * NF)
-    points, w0, w13, late, leaf_index, pair_index = together((points, w0, w13, late, leaf_index, pair_index))
+    points, w0, w1, late, leaf_index, pair_index = together((points, w0, w1, late, leaf_index, pair_index))
 
     states = lax.all_to_all(points, GROUP, split_axis=0, concat_axis=0, tiled=True)
-    w13 = pieces_from(w13, "x")
-    w1 = jnp.stack([piece[:, :128] for piece in w13])
-    w3 = jnp.stack([piece[:, 128:] for piece in w13])
+    w1 = jnp.stack(pieces_from(w1, "x"))
     w1 = jnp.stack(pieces_from(w1, "y"))
     w0 = jnp.stack(pieces_from(w0, "x"))
-    late = doubled(late, 16, zh // 2)
-    states = on_chip(select_body, states.shape, LONG, "leaves", leaf_index, states)
-    states, w0, w1, w3, late = together((states, w0, w1, w3, late))
-
-    far = flip(states, 1)
-    w2 = doubled(late, 32, zl)
-    joined, partial = near_step(0, "x", place, states, w0)
-    far, w2 = together((far, w2))
-    states = far_step(0, pair_index[0], far, joined, partial)
-
-    far = flip(states, 4)
-    states, w2 = together((states, w2))
-    w2 = jnp.stack(pieces_from(w2, "x"))
-    joined, partial = near_step(1, "y", place, states, w1)
-    far, w2 = together((far, w2))
-    states = far_step(1, pair_index[1], far, joined, partial)
-
-    far = flip(states, 16)
-    states, w3 = together((states, w3))
-    w3 = jnp.stack(pieces_from(w3, "y"))
-    joined, partial = near_step(2, "x", place, states, w2)
-    far, w3 = together((far, w3))
-    states = far_step(2, pair_index[2], far, joined, partial)
-
-    far = flip(states, 64)
-    joined, partial = near_step(3, "y", place, states, w3)
-    return far_step(3, pair_index[3], far, joined, partial)
+    states = on_chip(select_body, states.shape, SHORT, "leaves", leaf_index, states)
+    states, w0, w1 = together((states, w0, w1))
+
+    late = lax.all_gather(late, ("zh", "zl"))
+    others = {}
+    for level, mask in enumerate((1, 4, 16, 64)):
+        far = flip(states, mask)
+        if level == 2:
+            states, late = together((states, late))
+            others[2] = others[3] = flip(late, 1)
+        elif level < 2:
+            states, w1 = together((states, w1))
+            others[level] = flip((w0, w1)[level], 1)
+        joined, partial = near_step(level, place, states, [(w0, w1, late, late)[level]], [others[level]])
+        states = far_step(level, pair_index[level], far, joined, partial)
+    return states
 
 
 def solution(mesh):

time: 204 us -> 190 us (0.931)
  the two profiles are of different devices: /device:TPU:2 before, /device:TPU:66 now
where the time goes in v2:
time: 190 us; the launch traced here: 189 us
  waiting for transfers between devices  77.2 us (41%)
  starting transfers between devices  55.6 us (29%)
  Pallas kernels  20.7 us (11%)
  between operations  13.8 us (7%)
  other arithmetic  12 us (6%)
  matrix products  5.61 us (3%)
  local copies, waits for them, and re-layouts  4.37 us (2%)
    ppermute x10, waiting for transfers between devices, flip(): return lax.ppermute(value, AXES, [(i, i ^ mask) for i in range(size)])  50 us
    ppermute x12, starting transfers between devices, shifted(): return lax.ppermute(value, axis, [(i, (i + k) % size) for i in range(size)])  29.5 us
    ppermute x12, waiting for transfers between devices, shifted(): return lax.ppermute(value, axis, [(i, (i + k) % size) for i in range(size)])  24.4 us
    pallas_call x4, Pallas kernels, near_step(): pl.pallas_call(functools.partial(near_body, level, len(mine)), out_shape=...  15.3 us
    ppermute x10, starting transfers between devices, flip(): return lax.ppermute(value, AXES, [(i, i ^ mask) for i in range(size)])  12.2 us
    all_to_all x1, starting transfers between devices, on_device(): lax.all_to_all(points, GROUP, split_axis=0, concat_axis=0, tiled=True)  9.33 us
    dot_general x1, matrix products, on_device(): jnp.einsum('cb,kbt->kct', interp, traces.reshape(local_boxes, BOXT, local...  5.61 us
    pallas_call x6, Pallas kernels, on_chip(): pl.pallas_call(body, out_shape=jax.ShapeDtypeStruct(shape, BF16), in_spec...  5.39 us
  transfers between devices with their start and end apart: 25, of which 13 were waited for; matrix products, arithmetic and copies ran while one was open for 10% of the time, Pallas kernels for 9%

profile of v2, /device:TPU:66, one launch (start us, length us, event | category | flops | bytes accessed | tf_op | source)
XLA Modules:
  0.0 189.3 jit_solution(1917767052601884568)
XLA Ops:
  6.5 1.1 fusion.15
  7.7 0.7 fusion.13
  8.4 1.5 collective-permute-start.3
  9.9 1.1 collective-permute-start.4
  11.0 2.2 %collective-permute-start.5 = (bf16[2,64,512]{2,1,0:T(8,128)(2,1)}, bf16[2,64,512]{2,1,0:T(8,128)(2,1)}, u32[]{:S(2)}, u32[]{:S(2)}) collective-permute-start(bf16[2,64,512]{2,1,0:T(8,128)(2,1)} %get-tuple-element.74), channel_id=1, source_target_pairs={{0,192},{64,0},{128,64},{192,128},{1,193},{65,1},{129,65},{193,129... | collective-permute-start | bytes 393224 | tf_op jit(solution)/shard_map/ppermute | solution.py:46
  13.3 5.6 %convolution_convert_fusion = bf16[2048,128,2]{1,2,0:T(2,128)(2,1)} fusion(bf16[2048,16,128]{2,1,0:T(8,128)(2,1)} %bitcast.55, bf16[2,16]{1,0:T(2,128)(2,1)S(1)} %copy-done), kind=kOutput, calls=%fused_computation.2 | convolution fusion | flops 17301504 | bytes 9437248 | tf_op jit(solution)/shard_map/cb,kbt->kct/dot_general | solution.py:181
  19.4 6.9 %collective-permute-start.1 = (bf16[128,640]{1,0:T(8,128)(2,1)S(1)}, bf16[128,640]{1,0:T(8,128)(2,1)S(1)}, u32[]{:S(2)}, u32[]{:S(2)}) collective-permute-start(bf16[128,640]{1,0:T(8,128)(2,1)S(1)} %pad_maximum_fusion.6), channel_id=1, source_target_pairs={{0,16},{1,17},{2,18},{3,19},{4,20},{5,21},{6,22},{7,23},{8,24},{9,... | collective-permute-start | bytes 491528 | tf_op jit(solution)/shard_map/ppermute | solution.py:41
  26.6 4.5 %all-to-all-start = ((bf16[8,512,128]{2,1,0:T(8,128)(2,1)}), bf16[8,512,128]{2,1,0:T(8,128)(2,1)S(1)}, u32[]{:S(2)}, u32[]{:S(2)}) async-start(bf16[8,512,128]{2,1,0:T(8,128)(2,1)} %bitcast.6), calls=%async_computation | async-start | bytes 2097152 | tf_op jit(solution)/shard_map/all_to_all | solution.py:187
  31.2 1.7 collective-permute-done.1
  32.9 0.8 pad_maximum_fusion.5
  34.2 0.6 slice_bitcast_fusion
  34.9 2.0 %pad_maximum_fusion.3 = bf16[4,2,64,512]{3,2,1,0:T(8,128)(2,1)} fusion(bf16[1,2,64,512]{3,2,1,0:T(8,128)(2,1)} %bitcast.13, bf16[1,2,64,512]{3,2,1,0:T(8,128)(2,1)} %bitcast.12, bf16[1,2,64,512]{3,2,1,0:T(8,128)(2,1)} %bitcast.11, bf16[1,2,64,512]{3,2,1,0:T(8,128)(2,1)} %get-tuple-element.73), kind=kLoop, calls=%fused_computation.10 | loop fusion | flops 786432 | bytes 1048576 | tf_op jit(solution)/shard_map/stack | solution.py:177
  36.9 5.5 %collective-permute-done.2 = bf16[256,640]{1,0:T(8,128)(2,1)} collective-permute-done((bf16[256,640]{1,0:T(8,128)(2,1)}, bf16[256,640]{1,0:T(8,128)(2,1)}, u32[]{:S(2)}, u32[]{:S(2)}) %collective-permute-start.2) | collective-permute-done | bytes 327712 | tf_op jit(solution)/shard_map/ppermute | solution.py:41
  42.4 1.1 broadcast_select_fusion
  43.5 0.8 fusion
  44.3 2.8 %all-to-all-done = bf16[8,512,128]{2,1,0:T(8,128)(2,1)S(1)} async-done(((bf16[8,512,128]{2,1,0:T(8,128)(2,1)}), bf16[8,512,128]{2,1,0:T(8,128)(2,1)S(1)}, u32[]{:S(2)}, u32[]{:S(2)}) %all-to-all-start) | async-done | bytes 1048608 | tf_op jit(solution)/shard_map/all_to_all | solution.py:187
  47.2 0.7 spectrum.1
  48.0 1.0 reshape.149
  49.1 0.8 collective-permute-start.9
  49.9 9.3 %all-to-all-start.1 = ((bf16[32,8,1024]{2,1,0:T(8,128)(2,1)}), bf16[32,8,1024]{2,1,0:T(8,128)(2,1)S(1)}, u32[]{:S(2)}, u32[]{:S(2)}) async-start(bf16[32,8,1024]{2,1,0:T(8,128)(2,1)} %bitcast.19), calls=%async_computation.1 | async-start | bytes 1048576 | tf_op jit(solution)/shard_map/all_to_all | solution.py:197
  59.2 2.2 %collective-permute-start.10 = (bf16[512,128]{1,0:T(8,128)(2,1)S(1)}, bf16[512,128]{1,0:T(8,128)(2,1)S(1)}, u32[]{:S(2)}, u32[]{:S(2)}) collective-permute-start(bf16[512,128]{1,0:T(8,128)(2,1)S(1)} %pad_maximum_fusion.7), channel_id=1, source_target_pairs={{0,128},{64,192},{128,0},{192,64},{1,129},{65,193},{129,1},{193,65... | collective-permute-start | bytes 393224 | tf_op jit(solution)/shard_map/ppermute | solution.py:46
  61.4 1.4 collective-permute-start.11
  62.9 7.6 %collective-permute-done.9 = bf16[512,128]{1,0:T(8,128)(2,1)S(1)} collective-permute-done((bf16[512,128]{1,0:T(8,128)(2,1)S(1)}, bf16[512,128]{1,0:T(8,128)(2,1)S(1)}, u32[]{:S(2)}, u32[]{:S(2)}) %collective-permute-start.9) | collective-permute-done | bytes 131104 | tf_op jit(solution)/shard_map/ppermute | solution.py:46
  70.5 17.0 %collective-permute-start.8 = (bf16[512,512]{1,0:T(8,128)(2,1)S(1)}, bf16[512,512]{1,0:T(8,128)(2,1)S(1)}, u32[]{:S(2)}, u32[]{:S(2)}) collective-permute-start(bf16[512,512]{1,0:T(8,128)(2,1)S(1)} %copy-done.3), channel_id=1, source_target_pairs={{0,192},{64,0},{128,64},{192,128},{1,193},{65,1},{129,65},{193,129... | collective-permute-start | bytes 1572872 | tf_op jit(solution)/shard_map/ppermute | solution.py:46
  87.5 0.9 fusion.14
  88.9 2.1 %collective-permute-start.13 = (bf16[4,512,128]{2,1,0:T(8,128)(2,1)}, bf16[4,512,128]{2,1,0:T(8,128)(2,1)}, u32[]{:S(2)}, u32[]{:S(2)}) collective-permute-start(bf16[4,512,128]{2,1,0:T(8,128)(2,1)} %get-tuple-element.64), channel_id=1, source_target_pairs={{0,4},{2,6},{4,0},{6,2},{1,5},{3,7},{5,1},{7,3},{8,12},{10,14},{12... | collective-permute-start | bytes 1572872 | tf_op jit(solution)/shard_map/ppermute | solution.py:46
  91.0 0.7 collective-permute-start.14
  91.8 3.1 %collective-permute-done.8 = bf16[512,512]{1,0:T(8,128)(2,1)S(1)} collective-permute-done((bf16[512,512]{1,0:T(8,128)(2,1)S(1)}, bf16[512,512]{1,0:T(8,128)(2,1)S(1)}, u32[]{:S(2)}, u32[]{:S(2)}) %collective-permute-start.8) | collective-permute-done | bytes 524320 | tf_op jit(solution)/shard_map/ppermute | solution.py:46
  94.9 0.8 copy-done.5
  95.7 1.8 pad_maximum_fusion.refs_0_
  97.6 4.8 %collective-permute-done.12 = bf16[4,512,128]{2,1,0:T(8,128)(2,1)} collective-permute-done((bf16[4,512,128]{2,1,0:T(8,128)(2,1)}, bf16[4,512,128]{2,1,0:T(8,128)(2,1)}, u32[]{:S(2)}, u32[]{:S(2)}) %collective-permute-start.12) | collective-permute-done | bytes 524320 | tf_op jit(solution)/shard_map/ppermute | solution.py:46
  102.3 8.9 %collective-permute-done.13 = bf16[4,512,128]{2,1,0:T(8,128)(2,1)} collective-permute-done((bf16[4,512,128]{2,1,0:T(8,128)(2,1)}, bf16[4,512,128]{2,1,0:T(8,128)(2,1)}, u32[]{:S(2)}, u32[]{:S(2)}) %collective-permute-start.13) | collective-permute-done | bytes 524320 | tf_op jit(solution)/shard_map/ppermute | solution.py:46
  111.2 3.0 %pad_maximum_fusion.1.refs_0_ = bf16[4,4,512,128]{3,2,1,0:T(8,128)(2,1)} fusion(bf16[1,4,512,128]{3,2,1,0:T(8,128)(2,1)} %bitcast.32, bf16[1,4,512,128]{3,2,1,0:T(8,128)(2,1)} %bitcast.31, bf16[1,4,512,128]{3,2,1,0:T(8,128)(2,1)} %bitcast.30, bf16[1,4,512,128]{3,2,1,0:T(8,128)(2,1)S(1)} %get-tuple-element.63), kind=kLoop, calls=%fused_computation.1 | loop fusion | flops 3145728 | bytes 4194304 | tf_op jit(solution)/shard_map/stack | solution.py:199
  115.3 4.3 %collective-permute-done.16.refs_1_ = bf16[4,512,512]{2,1,0:T(8,128)(2,1)} collective-permute-done((bf16[4,512,512]{2,1,0:T(8,128)(2,1)S(1)}, bf16[4,512,512]{2,1,0:T(8,128)(2,1)}, u32[]{:S(2)}, u32[]{:S(2)}) %collective-permute-start.16) | collective-permute-done | bytes 2097184 | tf_op jit(solution)/shard_map/ppermute | solution.py:41
  119.7 3.5 %near0.1 = (bf16[2048,1024]{1,0:T(8,128)(2,1)S(1)}, f32[256,1024]{1,0:T(8,128)S(1)}) custom-call(s32[3]{0:T(128)S(1)} %pad_add_fusion.place, bf16[256,1024]{1,0:T(8,128)(2,1)S(1)} %leaves.1.own, bf16[4,512,512]{2,1,0:T(8,128)(2,1)} %copy-done.2, bf16[4,512,512]{2,1,0:T(8,128)(2,1)} %collective-permute-done.16.refs_1_), custom_call_target="tpu_custom_call" | custom-call | flops 536870912 | bytes 6291456 | tf_op jit(solution)/shard_map/near0/pallas_call | solution.py:146
  123.2 0.9 far0.1.own
  124.3 3.6 %collective-permute-start.17 = (bf16[256,1024]{1,0:T(8,128)(2,1)S(1)}, bf16[256,1024]{1,0:T(8,128)(2,1)S(1)}, u32[]{:S(2)}, u32[]{:S(2)}) collective-permute-start(bf16[256,1024]{1,0:T(8,128)(2,1)S(1)} %far0.1.own), channel_id=1, source_target_pairs={{0,4},{1,5},{2,6},{3,7},{4,0},{5,1},{6,2},{7,3},{8,12},{9,13},{10,... | collective-permute-start | bytes 1572872 | tf_op jit(solution)/shard_map/ppermute | solution.py:41
  128.0 0.6 collective-permute-done.18.refs_1_
  128.7 3.8 %near1.1 = (bf16[2048,1024]{1,0:T(8,128)(2,1)S(1)}, f32[256,1024]{1,0:T(8,128)S(1)}) custom-call(s32[3]{0:T(128)S(1)} %pad_add_fusion.place, bf16[256,1024]{1,0:T(8,128)(2,1)S(1)} %far0.1.own, bf16[4,4,512,128]{3,2,1,0:T(8,128)(2,1)} %pad_maximum_fusion.1.refs_0_, bf16[4,4,512,128]{3,2,1,0:T(8,128)(2,1)} %collective-permute-done.18.refs_1_), custom_call_target="tpu_custom_call" | custom-call | flops 536870912 | bytes 6291456 | tf_op jit(solution)/shard_map/near1/pallas_call | solution.py:146
  132.4 7.9 %collective-permute-done.17.far = bf16[256,1024]{1,0:T(8,128)(2,1)S(1)} collective-permute-done((bf16[256,1024]{1,0:T(8,128)(2,1)S(1)}, bf16[256,1024]{1,0:T(8,128)(2,1)S(1)}, u32[]{:S(2)}, u32[]{:S(2)}) %collective-permute-start.17) | collective-permute-done | bytes 524320 | tf_op jit(solution)/shard_map/ppermute | solution.py:41
  140.3 0.9 far1.1.own
  141.6 7.2 %collective-permute-done.20.refs_1_ = bf16[8,4,2,64,512]{4,3,2,1,0:T(8,128)(2,1)} collective-permute-done((bf16[8,4,2,64,512]{4,3,2,1,0:T(8,128)(2,1)}, bf16[8,4,2,64,512]{4,3,2,1,0:T(8,128)(2,1)}, u32[]{:S(2)}, u32[]{:S(2)}) %collective-permute-start.20) | collective-permute-done | bytes 4194336 | tf_op jit(solution)/shard_map/ppermute | solution.py:41
  148.8 4.0 %near2.1 = (bf16[2048,1024]{1,0:T(8,128)(2,1)S(1)}, f32[256,1024]{1,0:T(8,128)S(1)}) custom-call(s32[3]{0:T(128)S(1)} %pad_add_fusion.place, bf16[256,1024]{1,0:T(8,128)(2,1)S(1)} %far1.1.own, bf16[8,4,2,64,512]{4,3,2,1,0:T(8,128)(2,1)} %bitcast.57, bf16[8,4,2,64,512]{4,3,2,1,0:T(8,128)(2,1)} %collective-permute-done.20.refs_1_), custom_call_target="tpu_custom_call" | custom-call | flops 536870912 | bytes 6291456 | tf_op jit(solution)/shard_map/near2/pallas_call | solution.py:146
  152.9 13.0 %collective-permute-done.19.far = bf16[256,1024]{1,0:T(8,128)(2,1)S(1)} collective-permute-done((bf16[256,1024]{1,0:T(8,128)(2,1)S(1)}, bf16[256,1024]{1,0:T(8,128)(2,1)S(1)}, u32[]{:S(2)}, u32[]{:S(2)}) %collective-permute-start.19) | collective-permute-done | bytes 524320 | tf_op jit(solution)/shard_map/ppermute | solution.py:41
  165.9 0.9 far2.1.own
  167.0 4.0 %near3.1 = (bf16[2048,1024]{1,0:T(8,128)(2,1)S(1)}, f32[256,1024]{1,0:T(8,128)S(1)}) custom-call(s32[3]{0:T(128)S(1)} %pad_add_fusion.place, bf16[256,1024]{1,0:T(8,128)(2,1)S(1)} %far2.1.own, bf16[8,4,2,64,512]{4,3,2,1,0:T(8,128)(2,1)} %bitcast.58, bf16[8,4,2,64,512]{4,3,2,1,0:T(8,128)(2,1)} %collective-permute-done.20.refs_1_), custom_call_target="tpu_custom_call" | custom-call | flops 536870912 | bytes 6291456 | tf_op jit(solution)/shard_map/near3/pallas_call | solution.py:146
  171.0 9.7 %collective-permute-done.21.far = bf16[256,1024]{1,0:T(8,128)(2,1)S(1)} collective-permute-done((bf16[256,1024]{1,0:T(8,128)(2,1)S(1)}, bf16[256,1024]{1,0:T(8,128)(2,1)S(1)}, u32[]{:S(2)}, u32[]{:S(2)}) %collective-permute-start.21) | collective-permute-done | bytes 524320 | tf_op jit(solution)/shard_map/ppermute | solution.py:41
  180.7 1.7 far3.1
  (67 shorter events, 4.6 us)
Async XLA Ops:
  6.5 6.8 %copy-start = (bf16[2,16]{1,0:T(2,128)(2,1)S(1)}, bf16[2,16]{1,0:T(2,128)(2,1)}, u32[]{:S(2)}) copy-start(bf16[2,16]{1,0:T(2,128)(2,1)} %param.6) | copy-start | bytes 196
  8.4 26.5 %collective-permute-start.3 = (bf16[2,64,512]{2,1,0:T(8,128)(2,1)}, bf16[2,64,512]{2,1,0:T(8,128)(2,1)}, u32[]{:S(2)}, u32[]{:S(2)}) collective-permute-start(bf16[2,64,512]{2,1,0:T(8,128)(2,1)} %get-tuple-element.74), channel_id=1, source_target_pairs={{0,64},{64,128},{128,192},{192,0},{1,65},{65,129},{129,193},{193,1... | collective-permute-start | bytes 393224 | tf_op jit(solution)/shard_map/ppermute | solution.py:46
  9.9 25.0 %collective-permute-start.4 = (bf16[2,64,512]{2,1,0:T(8,128)(2,1)}, bf16[2,64,512]{2,1,0:T(8,128)(2,1)}, u32[]{:S(2)}, u32[]{:S(2)}) collective-permute-start(bf16[2,64,512]{2,1,0:T(8,128)(2,1)} %get-tuple-element.74), channel_id=1, source_target_pairs={{0,128},{64,192},{128,0},{192,64},{1,129},{65,193},{129,1},{193,65... | collective-permute-start | bytes 393224 | tf_op jit(solution)/shard_map/ppermute | solution.py:46
  11.0 23.9 %collective-permute-start.5 = (bf16[2,64,512]{2,1,0:T(8,128)(2,1)}, bf16[2,64,512]{2,1,0:T(8,128)(2,1)}, u32[]{:S(2)}, u32[]{:S(2)}) collective-permute-start(bf16[2,64,512]{2,1,0:T(8,128)(2,1)} %get-tuple-element.74), channel_id=1, source_target_pairs={{0,192},{64,0},{128,64},{192,128},{1,193},{65,1},{129,65},{193,129... | collective-permute-start | bytes 393224 | tf_op jit(solution)/shard_map/ppermute | solution.py:46
  13.2 6.1 %collective-permute-start = (bf16[64,640]{1,0:T(8,128)(2,1)S(1)}, bf16[64,640]{1,0:T(8,128)(2,1)S(1)}, u32[]{:S(2)}, u32[]{:S(2)}) collective-permute-start(bf16[64,640]{1,0:T(8,128)(2,1)S(1)} %pad_maximum_fusion.9), channel_id=1, source_target_pairs={{0,8},{1,9},{2,10},{3,11},{4,12},{5,13},{6,14},{7,15},{8,0},{9,1},... | collective-permute-start | bytes 245768 | tf_op jit(solution)/shard_map/ppermute | solution.py:41
  19.4 13.5 %collective-permute-start.1 = (bf16[128,640]{1,0:T(8,128)(2,1)S(1)}, bf16[128,640]{1,0:T(8,128)(2,1)S(1)}, u32[]{:S(2)}, u32[]{:S(2)}) collective-permute-start(bf16[128,640]{1,0:T(8,128)(2,1)S(1)} %pad_maximum_fusion.6), channel_id=1, source_target_pairs={{0,16},{1,17},{2,18},{3,19},{4,20},{5,21},{6,22},{7,23},{8,24},{9,... | collective-permute-start | bytes 491528 | tf_op jit(solution)/shard_map/ppermute | solution.py:41
  26.3 8.0 %copy-start.9 = (s32[4,256]{1,0:T(4,128)S(1)}, s32[4,256]{1,0:T(4,128)}, u32[]{:S(2)}) copy-start(s32[4,256]{1,0:T(4,128)} %param.9) | copy-start | bytes 12292
  26.6 20.4 %all-to-all-start = ((bf16[8,512,128]{2,1,0:T(8,128)(2,1)}), bf16[8,512,128]{2,1,0:T(8,128)(2,1)S(1)}, u32[]{:S(2)}, u32[]{:S(2)}) async-start(bf16[8,512,128]{2,1,0:T(8,128)(2,1)} %bitcast.6), calls=%async_computation | async-start | bytes 2097152 | tf_op jit(solution)/shard_map/all_to_all | solution.py:187
  31.1 110.1 %all-gather.3.cloned.1.call-start = ((), (), s32[]{:S(2)}) async-start(), calls=%async_computation.2 | async-start | bytes 4718592 | tf_op jit(solution)/shard_map/all_gather | solution.py:204
  33.7 8.7 %collective-permute-start.2 = (bf16[256,640]{1,0:T(8,128)(2,1)}, bf16[256,640]{1,0:T(8,128)(2,1)}, u32[]{:S(2)}, u32[]{:S(2)}) collective-permute-start(bf16[256,640]{1,0:T(8,128)(2,1)} %pad_maximum_fusion.5), channel_id=1, source_target_pairs={{0,32},{1,33},{2,34},{3,35},{4,36},{5,37},{6,38},{7,39},{8,40},{9,... | collective-permute-start | bytes 983048 | tf_op jit(solution)/shard_map/ppermute | solution.py:41
  47.2 1.7 copy-start.3
  48.0 43.7 %copy-start.10 = (s32[256]{0:T(256)S(1)}, s32[256]{0:T(256)}, u32[]{:S(2)}) copy-start(s32[256]{0:T(256)} %param.8) | copy-start | bytes 3076
  49.0 42.0 %collective-permute-start.6 = (bf16[512,512]{1,0:T(8,128)(2,1)S(1)}, bf16[512,512]{1,0:T(8,128)(2,1)}, u32[]{:S(2)}, u32[]{:S(2)}) collective-permute-start(bf16[512,512]{1,0:T(8,128)(2,1)S(1)} %copy-done.3), channel_id=1, source_target_pairs={{0,64},{64,128},{128,192},{192,0},{1,65},{65,129},{129,193},{193,1... | collective-permute-start | bytes 1572872 | tf_op jit(solution)/shard_map/ppermute | solution.py:46
  49.1 21.4 %collective-permute-start.9 = (bf16[512,128]{1,0:T(8,128)(2,1)S(1)}, bf16[512,128]{1,0:T(8,128)(2,1)S(1)}, u32[]{:S(2)}, u32[]{:S(2)}) collective-permute-start(bf16[512,128]{1,0:T(8,128)(2,1)S(1)} %pad_maximum_fusion.7), channel_id=1, source_target_pairs={{0,64},{64,128},{128,192},{192,0},{1,65},{65,129},{129,193},{193,1... | collective-permute-start | bytes 393224 | tf_op jit(solution)/shard_map/ppermute | solution.py:46
  49.9 64.3 %all-to-all-start.1 = ((bf16[32,8,1024]{2,1,0:T(8,128)(2,1)}), bf16[32,8,1024]{2,1,0:T(8,128)(2,1)S(1)}, u32[]{:S(2)}, u32[]{:S(2)}) async-start(bf16[32,8,1024]{2,1,0:T(8,128)(2,1)} %bitcast.19), calls=%async_computation.1 | async-start | bytes 1048576 | tf_op jit(solution)/shard_map/all_to_all | solution.py:197
  59.2 28.2 %collective-permute-start.10 = (bf16[512,128]{1,0:T(8,128)(2,1)S(1)}, bf16[512,128]{1,0:T(8,128)(2,1)S(1)}, u32[]{:S(2)}, u32[]{:S(2)}) collective-permute-start(bf16[512,128]{1,0:T(8,128)(2,1)S(1)} %pad_maximum_fusion.7), channel_id=1, source_target_pairs={{0,128},{64,192},{128,0},{192,64},{1,129},{65,193},{129,1},{193,65... | collective-permute-start | bytes 393224 | tf_op jit(solution)/shard_map/ppermute | solution.py:46
  61.4 26.0 %collective-permute-start.11 = (bf16[512,128]{1,0:T(8,128)(2,1)S(1)}, bf16[512,128]{1,0:T(8,128)(2,1)S(1)}, u32[]{:S(2)}, u32[]{:S(2)}) collective-permute-start(bf16[512,128]{1,0:T(8,128)(2,1)S(1)} %pad_maximum_fusion.7), channel_id=1, source_target_pairs={{0,192},{64,0},{128,64},{192,128},{1,193},{65,1},{129,65},{193,129... | collective-permute-start | bytes 393224 | tf_op jit(solution)/shard_map/ppermute | solution.py:46
  62.9 28.9 %collective-permute-start.7 = (bf16[512,512]{1,0:T(8,128)(2,1)S(1)}, bf16[512,512]{1,0:T(8,128)(2,1)S(1)}, u32[]{:S(2)}, u32[]{:S(2)}) collective-permute-start(bf16[512,512]{1,0:T(8,128)(2,1)S(1)} %copy-done.3), channel_id=1, source_target_pairs={{0,128},{64,192},{128,0},{192,64},{1,129},{65,193},{129,1},{193,65... | collective-permute-start | bytes 1572872 | tf_op jit(solution)/shard_map/ppermute | solution.py:46
  70.5 24.4 %collective-permute-start.8 = (bf16[512,512]{1,0:T(8,128)(2,1)S(1)}, bf16[512,512]{1,0:T(8,128)(2,1)S(1)}, u32[]{:S(2)}, u32[]{:S(2)}) collective-permute-start(bf16[512,512]{1,0:T(8,128)(2,1)S(1)} %copy-done.3), channel_id=1, source_target_pairs={{0,192},{64,0},{128,64},{192,128},{1,193},{65,1},{129,65},{193,129... | collective-permute-start | bytes 1572872 | tf_op jit(solution)/shard_map/ppermute | solution.py:46
  88.4 14.0 %collective-permute-start.12 = (bf16[4,512,128]{2,1,0:T(8,128)(2,1)}, bf16[4,512,128]{2,1,0:T(8,128)(2,1)}, u32[]{:S(2)}, u32[]{:S(2)}) collective-permute-start(bf16[4,512,128]{2,1,0:T(8,128)(2,1)} %get-tuple-element.64), channel_id=1, source_target_pairs={{0,2},{2,4},{4,6},{6,0},{1,3},{3,5},{5,7},{7,1},{8,10},{10,12},{12... | collective-permute-start | bytes 1572872 | tf_op jit(solution)/shard_map/ppermute | solution.py:46
  88.9 22.3 %collective-permute-start.13 = (bf16[4,512,128]{2,1,0:T(8,128)(2,1)}, bf16[4,512,128]{2,1,0:T(8,128)(2,1)}, u32[]{:S(2)}, u32[]{:S(2)}) collective-permute-start(bf16[4,512,128]{2,1,0:T(8,128)(2,1)} %get-tuple-element.64), channel_id=1, source_target_pairs={{0,4},{2,6},{4,0},{6,2},{1,5},{3,7},{5,1},{7,3},{8,12},{10,14},{12... | collective-permute-start | bytes 1572872 | tf_op jit(solution)/shard_map/ppermute | solution.py:46
  91.0 20.2 %collective-permute-start.14 = (bf16[4,512,128]{2,1,0:T(8,128)(2,1)}, bf16[4,512,128]{2,1,0:T(8,128)(2,1)}, u32[]{:S(2)}, u32[]{:S(2)}) collective-permute-start(bf16[4,512,128]{2,1,0:T(8,128)(2,1)} %get-tuple-element.64), channel_id=1, source_target_pairs={{0,6},{2,0},{4,2},{6,4},{1,7},{3,1},{5,3},{7,5},{8,14},{10,8},{12,... | collective-permute-start | bytes 1572872 | tf_op jit(solution)/shard_map/ppermute | solution.py:46
  91.8 3.1 %copy-start.4 = (bf16[512,512]{1,0:T(8,128)(2,1)}, bf16[512,512]{1,0:T(8,128)(2,1)S(1)}, u32[]{:S(2)}) copy-start(bf16[512,512]{1,0:T(8,128)(2,1)S(1)} %collective-permute-done.7) | copy-start | bytes 1572868
  94.9 0.8 copy-start.5
  97.6 17.0 %copy-start.2 = (bf16[4,512,512]{2,1,0:T(8,128)(2,1)}, bf16[4,512,512]{2,1,0:T(8,128)(2,1)S(1)}, u32[]{:S(2)}) copy-start(bf16[4,512,512]{2,1,0:T(8,128)(2,1)S(1)} %pad_maximum_fusion.refs_0_) | copy-start | bytes 6291460
  114.5 5.1 %collective-permute-start.16 = (bf16[4,512,512]{2,1,0:T(8,128)(2,1)S(1)}, bf16[4,512,512]{2,1,0:T(8,128)(2,1)}, u32[]{:S(2)}, u32[]{:S(2)}) collective-permute-start(bf16[4,512,512]{2,1,0:T(8,128)(2,1)S(1)} %pad_maximum_fusion.refs_0_), channel_id=1, source_target_pairs={{0,1},{1,0},{2,3},{3,2},{4,5},{5,4},{6,7},{7,6},{8,9},{9,8},{10,11... | collective-permute-start | bytes 6291464 | tf_op jit(solution)/shard_map/ppermute | solution.py:41
  114.6 8.5 %collective-permute-start.15 = (bf16[256,1024]{1,0:T(8,128)(2,1)S(1)}, bf16[256,1024]{1,0:T(8,128)(2,1)S(1)}, u32[]{:S(2)}, u32[]{:S(2)}) collective-permute-start(bf16[256,1024]{1,0:T(8,128)(2,1)S(1)} %leaves.1.own), channel_id=1, source_target_pairs={{0,1},{1,0},{2,3},{3,2},{4,5},{5,4},{6,7},{7,6},{8,9},{9,8},{10,11... | collective-permute-start | bytes 1572872 | tf_op jit(solution)/shard_map/ppermute | solution.py:41
  123.2 4.7 %copy-start.8 = (s32[256,1]{0,1:T(1,128)S(1)}, s32[256,1]{0,1:T(1,128)}, u32[]{:S(2)}) copy-start(s32[256,1]{0,1:T(1,128)} %get-tuple-element.37) | copy-start | bytes 3076
  124.1 4.6 %collective-permute-start.18 = (bf16[4,4,512,128]{3,2,1,0:T(8,128)(2,1)}, bf16[4,4,512,128]{3,2,1,0:T(8,128)(2,1)}, u32[]{:S(2)}, u32[]{:S(2)}) collective-permute-start(bf16[4,4,512,128]{3,2,1,0:T(8,128)(2,1)} %pad_maximum_fusion.1.refs_0_), channel_id=1, source_target_pairs={{0,1},{1,0},{2,3},{3,2},{4,5},{5,4},{6,7},{7,6},{8,9},{9,8},{10,11... | collective-permute-start | bytes 6291464 | tf_op jit(solution)/shard_map/ppermute | solution.py:41
  124.3 16.0 %collective-permute-start.17 = (bf16[256,1024]{1,0:T(8,128)(2,1)S(1)}, bf16[256,1024]{1,0:T(8,128)(2,1)S(1)}, u32[]{:S(2)}, u32[]{:S(2)}) collective-permute-start(bf16[256,1024]{1,0:T(8,128)(2,1)S(1)} %far0.1.own), channel_id=1, source_target_pairs={{0,4},{1,5},{2,6},{3,7},{4,0},{5,1},{6,2},{7,3},{8,12},{9,13},{10,... | collective-permute-start | bytes 1572872 | tf_op jit(solution)/shard_map/ppermute | solution.py:41
  140.3 1.1 copy-start.7
  141.2 7.6 %collective-permute-start.20 = (bf16[8,4,2,64,512]{4,3,2,1,0:T(8,128)(2,1)}, bf16[8,4,2,64,512]{4,3,2,1,0:T(8,128)(2,1)}, u32[]{:S(2)}, u32[]{:S(2)}) collective-permute-start(bf16[8,4,2,64,512]{4,3,2,1,0:T(8,128)(2,1)} %bitcast.56), channel_id=1, source_target_pairs={{0,1},{1,0},{2,3},{3,2},{4,5},{5,4},{6,7},{7,6},{8,9},{9,8},{10,11... | collective-permute-start | bytes 12582920 | tf_op jit(solution)/shard_map/ppermute | solution.py:41
  141.3 24.5 %collective-permute-start.19 = (bf16[256,1024]{1,0:T(8,128)(2,1)S(1)}, bf16[256,1024]{1,0:T(8,128)(2,1)S(1)}, u32[]{:S(2)}, u32[]{:S(2)}) collective-permute-start(bf16[256,1024]{1,0:T(8,128)(2,1)S(1)} %far1.1.own), channel_id=1, source_target_pairs={{0,16},{1,17},{2,18},{3,19},{4,20},{5,21},{6,22},{7,23},{8,24},{9,... | collective-permute-start | bytes 1572872 | tf_op jit(solution)/shard_map/ppermute | solution.py:41
  165.9 1.0 copy-start.6
  166.8 14.0 %collective-permute-start.21 = (bf16[256,1024]{1,0:T(8,128)(2,1)S(1)}, bf16[256,1024]{1,0:T(8,128)(2,1)S(1)}, u32[]{:S(2)}, u32[]{:S(2)}) collective-permute-start(bf16[256,1024]{1,0:T(8,128)(2,1)S(1)} %far2.1.own), channel_id=1, source_target_pairs={{0,64},{1,65},{2,66},{3,67},{4,68},{5,69},{6,70},{7,71},{8,72},{9,... | collective-permute-start | bytes 1572872 | tf_op jit(solution)/shard_map/ppermute | solution.py:41
  180.7 1.7 copy-start.1
Sparse Core Ops, SparseCore 0:
  49.1 61.8 all-gather.2

commit v3 on v2

--- a/solution.py
+++ b/solution.py
@@ -67,35 +67,24 @@
 
 
 def plan_copies(level, place, mine, other, weights):
-    x, y, c = place[0], place[1], place[2]
+    x, c = place[0], place[1]
     copies = []
-    for half, sources in enumerate((mine, other)):
-        column = jnp.where(c == half, 0, 512)
-        for source in sources:
-            if len(source.shape) == 5:
-                cols = pl.ds(pl.multiple_of(column, 512), 512)
-                for n in range(4):
-                    for z in range(8):
-                        row = lax.rem(x + (4 - n), 4) * 512 + (z % 2 * 4 + z // 2) * 64
-                        rows = pl.ds(pl.multiple_of(row, 64), 64)
-                        copies.append((source.at[z, n, level - 2], weights.at[rows, cols]))
+    for half, source in enumerate((mine, other)):
+        cols = pl.ds(pl.multiple_of(jnp.where(c == half, 0, 512), 512), 512)
         for k in range(4):
-            rows = pl.ds(pl.multiple_of(lax.rem(x + (4 - k), 4) * 512, 512), 512)
-            for n, source in enumerate(sources):
-                if len(source.shape) == 3:
-                    width = source.shape[2]
-                    cols = pl.ds(pl.multiple_of(column + n * width, 256), width)
-                    copies.append((source.at[k], weights.at[rows, cols]))
-                elif len(source.shape) == 4:
-                    for j in range(4):
-                        cols = pl.ds(pl.multiple_of(column + lax.rem(y + (4 - j), 4) * 128, 128), 128)
-                        copies.append((source.at[j, k], weights.at[rows, cols]))
+            start = lax.rem(x + (4 - k), 4) * 512
+            if len(source.shape) == 3:
+                rows = pl.ds(pl.multiple_of(start, 512), 512)
+                copies.append((source.at[k], weights.at[rows, cols]))
+                continue
+            for z in range(8):
+                rows = pl.ds(pl.multiple_of(start + (z % 2 * 4 + z // 2) * 64, 64), 64)
+                block = source.at[z, k] if level == 1 else source.at[z, k, level - 2]
+                copies.append((block, weights.at[rows, cols]))
     return copies
 
 
-def near_body(level, count, place, own, *refs):
-    mine, other = refs[:count], refs[count : 2 * count]
-    weights, partial, sems = refs[2 * count :]
+def near_body(level, place, own, mine, other, weights, partial, sems):
     started = []
     for n, (source, target) in enumerate(plan_copies(level, place, mine, other, weights)):
         copy = pltpu.make_async_copy(source, target, sems.at[n])
@@ -116,6 +105,10 @@
         out[:, cols] = (total + partial[:, cols]).astype(BF16)
 
 
+def copy_body(values, out):
+    out[...] = values[...]
+
+
 def select_body(index, values, out):
     out[...] = select_rows(index[...], values[...])
 
@@ -141,18 +134,18 @@
 
 
 def near_step(level, place, own, mine, other):
-    pieces = [pltpu.with_memory_space_constraint(piece, pltpu.HBM) for piece in (*mine, *other)]
-    copies = sum({5: 32, 3: 4, 4: 16}[piece.ndim] for piece in pieces)
+    mine, other = [pltpu.with_memory_space_constraint(piece, pltpu.HBM) for piece in (mine, other)]
+    copies = 8 if mine.ndim == 3 else 64
     return pl.pallas_call(
-        functools.partial(near_body, level, len(mine)),
+        functools.partial(near_body, level),
         out_shape=[jax.ShapeDtypeStruct((2048, 1024), BF16), jax.ShapeDtypeStruct(own.shape, F32)],
-        in_specs=[pl.BlockSpec(memory_space=pltpu.SMEM), VMEM] + [HBM] * len(pieces),
+        in_specs=[pl.BlockSpec(memory_space=pltpu.SMEM), VMEM, HBM, HBM],
         out_specs=[VMEM, VMEM],
         scratch_shapes=[pltpu.SemaphoreType.DMA((copies,))],
         compiler_params=pltpu.CompilerParams(vmem_limit_bytes=VMEM_LIMIT),
         cost_estimate=pl.CostEstimate(flops=256 * 2048 * 1024, bytes_accessed=6 << 20, transcendentals=0),
         name="near" + str(level),
-    )(place, own, *pieces)
+    )(place, own, mine, other)
 
 
 def far_step(level, index, far, joined, partial):
@@ -160,58 +153,54 @@
 
 
 def on_device(traces, interp, translations, leaf_slot, pairing):
-    x, y, c = lax.axis_index("x"), lax.axis_index("y"), lax.axis_index("c")
+    x, c = lax.axis_index("x"), lax.axis_index("c")
     zl, zh = lax.axis_index("zl"), lax.axis_index("zh")
     together = lax.optimization_barrier
-    place = jnp.stack([x, y, c]).astype(jnp.int32)
+    place = jnp.stack([x, c]).astype(jnp.int32)
 
     def column(values):
         return values.reshape(values.shape[0], 1)
 
-    def half(level):
-        return lax.dynamic_slice_in_dim(translations[level], c * 512, 512, 1)
-
-    def eighth(level):
-        return lax.dynamic_slice_in_dim(translations[level], c * 512 + y * 128, 128, 1)
-
-    late = jnp.stack(pieces_from(jnp.stack([half(2), half(3)]), "x"))
-    rows = doubled(jnp.concatenate([half(0), eighth(1)], axis=1), 8, zh % 2)
+    half = lax.dynamic_slice_in_dim(translations, c * 512, 512, 2)
+    late = pieces_from(half[1:], "x")
+    rows = doubled(half[0], 8, zh % 2)
     local_boxes = traces.shape[0] // BOXT
     local_cols = traces.shape[1]
     sampled = jnp.einsum(
         "cb,kbt->kct", interp, traces.reshape(local_boxes, BOXT, local_cols), preferred_element_type=F32
     )
     sampled = sampled.astype(BF16).reshape(local_boxes * CHEB, local_cols)
-    sampled, rows = together((sampled, rows))
+    sampled, rows, late = together((sampled, rows, late))
+    late = jnp.stack(late)
 
     sampled = lax.all_to_all(sampled, TA, split_axis=0, concat_axis=1, tiled=True)
-    rows = doubled(doubled(rows, 16, zh // 2), 32, zl)
-    w0, w1 = rows[:, :512], rows[:, 512:]
+    w0 = doubled(doubled(rows, 16, zh // 2), 32, zl)
     fourier = spectrum_table(sampled.shape[1], NF)
     leaf_index, *pair_index = [column(values) for values in (leaf_slot, *pairing)]
     points = on_chip(
         spectrum_body, (sampled.shape[0], fourier.shape[1]), LONG, "spectrum", sampled, fourier
     ).reshape(sampled.shape[0] // CHEB, CHEB * 2 * NF)
-    points, w0, w1, late, leaf_index, pair_index = together((points, w0, w1, late, leaf_index, pair_index))
+    points, w0, leaf_index, pair_index = together((points, w0, leaf_index, pair_index))
 
     states = lax.all_to_all(points, GROUP, split_axis=0, concat_axis=0, tiled=True)
-    w1 = jnp.stack(pieces_from(w1, "x"))
-    w1 = jnp.stack(pieces_from(w1, "y"))
+    w1 = lax.all_gather(late[:, 0], ("zh", "zl"))
     w0 = jnp.stack(pieces_from(w0, "x"))
     states = on_chip(select_body, states.shape, SHORT, "leaves", leaf_index, states)
     states, w0, w1 = together((states, w0, w1))
 
-    late = lax.all_gather(late, ("zh", "zl"))
-    others = {}
+    w23 = lax.all_gather(late[:, 1:], ("zh", "zl"))
+    others = {0: flip(w0, 1)}
     for level, mask in enumerate((1, 4, 16, 64)):
         far = flip(states, mask)
+        if level == 1:
+            states, w1 = together((states, w1))
+            others[1] = flip(w1, 1)
+        elif level == 2:
+            states, w23 = together((states, w23))
+            others[2] = others[3] = flip(w23, 1)
+        joined, partial = near_step(level, place, states, (w0, w1, w23, w23)[level], others[level])
         if level == 2:
-            states, late = together((states, late))
-            others[2] = others[3] = flip(late, 1)
-        elif level < 2:
-            states, w1 = together((states, w1))
-            others[level] = flip((w0, w1)[level], 1)
-        joined, partial = near_step(level, place, states, [(w0, w1, late, late)[level]], [others[level]])
+            far = on_chip(copy_body, far.shape, LONG, "arrived2", far)
         states = far_step(level, pair_index[level], far, joined, partial)
     return states
 

time: 190 us -> 186 us (0.979)
  the two profiles are of different devices: /device:TPU:66 before, /device:TPU:128 now
where the time goes in v3:
time: 186 us; the launch traced here: 185 us
  waiting for transfers between devices  93.5 us (50%)
  starting transfers between devices  36.6 us (20%)
  Pallas kernels  21.1 us (11%)
  between operations  13.8 us (7%)
  local copies, waits for them, and re-layouts  7.58 us (4%)
  other arithmetic  7.03 us (4%)
  matrix products  5.6 us (3%)
    ppermute x10, waiting for transfers between devices, flip(): return lax.ppermute(value, AXES, [(i, i ^ mask) for i in range(size)])  40.9 us
    all_gather x1, waiting for transfers between devices, on_device(): w23 = lax.all_gather(late[:, 1:], ('zh', 'zl'))  29 us
    ppermute x6, waiting for transfers between devices, shifted(): return lax.ppermute(value, axis, [(i, (i + k) % size) for i in range(size)])  23.5 us
    pallas_call x4, Pallas kernels, near_step(): pl.pallas_call(functools.partial(near_body, level), out_shape=[jax.ShapeD...  15.7 us
    ppermute x6, starting transfers between devices, shifted(): return lax.ppermute(value, axis, [(i, (i + k) % size) for i in range(size)])  11.4 us
    ppermute x10, starting transfers between devices, flip(): return lax.ppermute(value, AXES, [(i, i ^ mask) for i in range(size)])  11.2 us
    all_to_all x1, starting transfers between devices, on_device(): lax.all_to_all(points, GROUP, split_axis=0, concat_axis=0, tiled=True)  9.41 us
    dot_general x1, matrix products, on_device(): jnp.einsum('cb,kbt->kct', interp, traces.reshape(local_boxes, BOXT, local...  5.6 us
  transfers between devices with their start and end apart: 20, of which 10 were waited for; matrix products, arithmetic and copies ran while one was open for 8% of the time, Pallas kernels for 8%

profile of v3, /device:TPU:128, one launch (start us, length us, event | category | flops | bytes accessed | tf_op | source)
XLA Modules:
  0.0 185.2 jit_solution(11982376027086096155)
XLA Ops:
  6.5 1.0 constant_dynamic-slice_fusion
  7.5 1.6 collective-permute-start.1
  9.1 2.7 %collective-permute-start.2 = (bf16[3,64,512]{2,1,0:T(8,128)(2,1)S(1)}, bf16[3,64,512]{2,1,0:T(8,128)(2,1)S(1)}, u32[]{:S(2)}, u32[]{:S(2)}) collective-permute-start(bf16[3,64,512]{2,1,0:T(8,128)(2,1)S(1)} %constant_dynamic-slice_fusion), channel_id=1, source_target_pairs={{0,128},{64,192},{128,0},{192,64},{1,129},{65,193},{129,1},{193,65... | collective-permute-start | bytes 589832 | tf_op jit(solution)/shard_map/ppermute | solution.py:46
  11.8 1.4 collective-permute-start.3
  13.2 0.8 dynamic-slice_bitcast_fusion
  14.1 1.5 collective-permute-start
  15.5 5.6 %convolution_convert_fusion = bf16[2048,128,2]{1,2,0:T(2,128)(2,1)} fusion(bf16[2048,16,128]{2,1,0:T(8,128)(2,1)} %bitcast.45, bf16[2,16]{1,0:T(2,128)(2,1)S(1)} %copy-done), kind=kOutput, calls=%fused_computation.1 | convolution fusion | flops 17301504 | bytes 9437248 | tf_op jit(solution)/shard_map/cb,kbt->kct/dot_general | solution.py:169
  21.2 0.9 broadcast_select_fusion.5
  22.1 0.9 pad_maximum_fusion.6
  23.4 0.4 subtract_convert_fusion
  23.8 0.6 collective-permute-start.4
  24.4 0.5 slice_bitcast_fusion
  25.0 4.5 %all-to-all-start = ((bf16[8,512,128]{2,1,0:T(8,128)(2,1)}), bf16[8,512,128]{2,1,0:T(8,128)(2,1)S(1)}, u32[]{:S(2)}, u32[]{:S(2)}) async-start(bf16[8,512,128]{2,1,0:T(8,128)(2,1)} %bitcast.5), calls=%async_computation | async-start | bytes 2097152 | tf_op jit(solution)/shard_map/all_to_all | solution.py:176
  29.5 3.5 %collective-permute-done.4 = bf16[128,512]{1,0:T(8,128)(2,1)S(1)} collective-permute-done((bf16[128,512]{1,0:T(8,128)(2,1)S(1)}, bf16[128,512]{1,0:T(8,128)(2,1)S(1)}, u32[]{:S(2)}, u32[]{:S(2)}) %collective-permute-start.4) | collective-permute-done | bytes 131104 | tf_op jit(solution)/shard_map/ppermute | solution.py:41
  33.0 0.7 pad_maximum_fusion.7
  33.8 2.4 %collective-permute-start.5 = (bf16[256,512]{1,0:T(8,128)(2,1)}, bf16[256,512]{1,0:T(8,128)(2,1)}, u32[]{:S(2)}, u32[]{:S(2)}) collective-permute-start(bf16[256,512]{1,0:T(8,128)(2,1)} %pad_maximum_fusion.7), channel_id=1, source_target_pairs={{0,32},{1,33},{2,34},{3,35},{4,36},{5,37},{6,38},{7,39},{8,40},{9,... | collective-permute-start | bytes 786440 | tf_op jit(solution)/shard_map/ppermute | solution.py:41
  36.3 0.9 pad_maximum_fusion.2
  37.2 11.1 %collective-permute-done.5 = bf16[256,512]{1,0:T(8,128)(2,1)} collective-permute-done((bf16[256,512]{1,0:T(8,128)(2,1)}, bf16[256,512]{1,0:T(8,128)(2,1)}, u32[]{:S(2)}, u32[]{:S(2)}) %collective-permute-start.5) | collective-permute-done | bytes 262176 | tf_op jit(solution)/shard_map/ppermute | solution.py:41
  48.3 1.1 broadcast_select_fusion.1
  49.6 0.7 spectrum.1
  50.3 1.0 reshape.143
  51.2 9.4 %all-to-all-start.1 = ((bf16[32,8,1024]{2,1,0:T(8,128)(2,1)}), bf16[32,8,1024]{2,1,0:T(8,128)(2,1)S(1)}, u32[]{:S(2)}, u32[]{:S(2)}) async-start(bf16[32,8,1024]{2,1,0:T(8,128)(2,1)} %bitcast.14), calls=%async_computation.1 | async-start | bytes 1048576 | tf_op jit(solution)/shard_map/all_to_all | solution.py:185
  60.7 1.5 collective-permute-start.6
  62.2 2.7 %collective-permute-start.7 = (bf16[512,512]{1,0:T(8,128)(2,1)S(1)}, bf16[512,512]{1,0:T(8,128)(2,1)S(1)}, u32[]{:S(2)}, u32[]{:S(2)}) collective-permute-start(bf16[512,512]{1,0:T(8,128)(2,1)S(1)} %pad_maximum_fusion.5), channel_id=1, source_target_pairs={{0,128},{64,192},{128,0},{192,64},{1,129},{65,193},{129,1},{193,65... | collective-permute-start | bytes 1572872 | tf_op jit(solution)/shard_map/ppermute | solution.py:46
  64.9 1.4 collective-permute-start.8
  66.5 13.9 %collective-permute-done.6 = bf16[512,512]{1,0:T(8,128)(2,1)S(1)} collective-permute-done((bf16[512,512]{1,0:T(8,128)(2,1)S(1)}, bf16[512,512]{1,0:T(8,128)(2,1)S(1)}, u32[]{:S(2)}, u32[]{:S(2)}) %collective-permute-start.6) | collective-permute-done | bytes 524320 | tf_op jit(solution)/shard_map/ppermute | solution.py:46
  80.4 9.6 %collective-permute-done.7 = bf16[512,512]{1,0:T(8,128)(2,1)S(1)} collective-permute-done((bf16[512,512]{1,0:T(8,128)(2,1)S(1)}, bf16[512,512]{1,0:T(8,128)(2,1)S(1)}, u32[]{:S(2)}, u32[]{:S(2)}) %collective-permute-start.7) | collective-permute-done | bytes 524320 | tf_op jit(solution)/shard_map/ppermute | solution.py:46
  90.0 1.7 pad_maximum_fusion.mine
  92.1 0.5 collective-permute-start.9
  92.8 3.9 %collective-permute-done.10.other = bf16[4,512,512]{2,1,0:T(8,128)(2,1)} collective-permute-done((bf16[4,512,512]{2,1,0:T(8,128)(2,1)}, bf16[4,512,512]{2,1,0:T(8,128)(2,1)}, u32[]{:S(2)}, u32[]{:S(2)}) %collective-permute-start.10) | collective-permute-done | bytes 2097184 | tf_op jit(solution)/shard_map/ppermute | solution.py:41
  96.8 3.5 %near0.1 = (bf16[2048,1024]{1,0:T(8,128)(2,1)S(1)}, f32[256,1024]{1,0:T(8,128)S(1)}) custom-call(s32[2]{0:T(128)S(1)} %pad_add_fusion.place, bf16[256,1024]{1,0:T(8,128)(2,1)S(1)} %leaves.1.own, bf16[4,512,512]{2,1,0:T(8,128)(2,1)} %pad_maximum_fusion.mine, bf16[4,512,512]{2,1,0:T(8,128)(2,1)} %collective-permute-done.10.other), custom_call_target="tpu_custom_call" | custom-call | flops 536870912 | bytes 6291456 | tf_op jit(solution)/shard_map/near0/pallas_call | solution.py:139
  100.3 0.9 far0.1.own
  101.4 3.3 %collective-permute-start.11 = (bf16[256,1024]{1,0:T(8,128)(2,1)S(1)}, bf16[256,1024]{1,0:T(8,128)(2,1)S(1)}, u32[]{:S(2)}, u32[]{:S(2)}) collective-permute-start(bf16[256,1024]{1,0:T(8,128)(2,1)S(1)} %far0.1.own), channel_id=1, source_target_pairs={{0,4},{1,5},{2,6},{3,7},{4,0},{5,1},{6,2},{7,3},{8,12},{9,13},{10,... | collective-permute-start | bytes 1572872 | tf_op jit(solution)/shard_map/ppermute | solution.py:41
  104.9 0.8 collective-permute-done.12.other
  105.7 1.4 copy-done.2
  107.1 4.1 %near1.1 = (bf16[2048,1024]{1,0:T(8,128)(2,1)S(1)}, f32[256,1024]{1,0:T(8,128)S(1)}) custom-call(s32[2]{0:T(128)S(1)} %pad_add_fusion.place, bf16[256,1024]{1,0:T(8,128)(2,1)S(1)} %far0.1.own, bf16[8,4,64,512]{3,2,1,0:T(8,128)(2,1)} %bitcast.24.mine, bf16[8,4,64,512]{3,2,1,0:T(8,128)(2,1)} %copy-done.2), custom_call_target="tpu_custom_call" | custom-call | flops 536870912 | bytes 6291456 | tf_op jit(solution)/shard_map/near1/pallas_call | solution.py:139
  111.1 6.1 %collective-permute-done.11.far = bf16[256,1024]{1,0:T(8,128)(2,1)S(1)} collective-permute-done((bf16[256,1024]{1,0:T(8,128)(2,1)S(1)}, bf16[256,1024]{1,0:T(8,128)(2,1)S(1)}, u32[]{:S(2)}, u32[]{:S(2)}) %collective-permute-start.11) | collective-permute-done | bytes 524320 | tf_op jit(solution)/shard_map/ppermute | solution.py:41
  117.2 0.9 far1.1.own
  118.1 1.0 collective-permute-start.13
  119.2 29.0 %all-gather.7.cloned.1.call-done = bf16[32,2,64,512]{3,2,1,0:T(8,128)(2,1)} async-done(((bf16[4,2,64,512]{3,2,1,0:T(8,128)(2,1)}), bf16[32,2,64,512]{3,2,1,0:T(8,128)(2,1)}) %all-gather.7.cloned.1.call-update) | async-done | bytes 4194320 | tf_op jit(solution)/shard_map/all_gather | solution.py:191
  148.3 7.3 %collective-permute-done.14.other = bf16[8,4,2,64,512]{4,3,2,1,0:T(8,128)(2,1)S(1)} collective-permute-done((bf16[8,4,2,64,512]{4,3,2,1,0:T(8,128)(2,1)}, bf16[8,4,2,64,512]{4,3,2,1,0:T(8,128)(2,1)S(1)}, u32[]{:S(2)}, u32[]{:S(2)}) %collective-permute-start.14) | collective-permute-done | bytes 4194336 | tf_op jit(solution)/shard_map/ppermute | solution.py:41
  155.6 2.0 %copy-done.1 = bf16[8,4,2,64,512]{4,3,2,1,0:T(8,128)(2,1)} copy-done((bf16[8,4,2,64,512]{4,3,2,1,0:T(8,128)(2,1)}, bf16[8,4,2,64,512]{4,3,2,1,0:T(8,128)(2,1)S(1)}, u32[]{:S(2)}) %copy-start.1) | copy-done | bytes 4194328
  157.6 4.0 %near2.1 = (bf16[2048,1024]{1,0:T(8,128)(2,1)S(1)}, f32[256,1024]{1,0:T(8,128)S(1)}) custom-call(s32[2]{0:T(128)S(1)} %pad_add_fusion.place, bf16[256,1024]{1,0:T(8,128)(2,1)S(1)} %far1.1.own, bf16[8,4,2,64,512]{4,3,2,1,0:T(8,128)(2,1)} %bitcast.47, bf16[8,4,2,64,512]{4,3,2,1,0:T(8,128)(2,1)} %copy-done.1), custom_call_target="tpu_custom_call" | custom-call | flops 536870912 | bytes 6291456 | tf_op jit(solution)/shard_map/near2/pallas_call | solution.py:139
  161.7 0.9 far2.1.own
  162.6 1.6 collective-permute-start.15
  164.3 4.1 %near3.1 = (bf16[2048,1024]{1,0:T(8,128)(2,1)S(1)}, f32[256,1024]{1,0:T(8,128)S(1)}) custom-call(s32[2]{0:T(128)S(1)} %pad_add_fusion.place, bf16[256,1024]{1,0:T(8,128)(2,1)S(1)} %far2.1.own, bf16[8,4,2,64,512]{4,3,2,1,0:T(8,128)(2,1)} %bitcast.48, bf16[8,4,2,64,512]{4,3,2,1,0:T(8,128)(2,1)} %copy-done.1), custom_call_target="tpu_custom_call" | custom-call | flops 536870912 | bytes 6291456 | tf_op jit(solution)/shard_map/near3/pallas_call | solution.py:139
  168.4 8.3 %collective-permute-done.15.far = bf16[256,1024]{1,0:T(8,128)(2,1)S(1)} collective-permute-done((bf16[256,1024]{1,0:T(8,128)(2,1)S(1)}, bf16[256,1024]{1,0:T(8,128)(2,1)S(1)}, u32[]{:S(2)}, u32[]{:S(2)}) %collective-permute-start.15) | collective-permute-done | bytes 524320 | tf_op jit(solution)/shard_map/ppermute | solution.py:41
  176.6 1.7 far3.1
  (61 shorter events, 2.2 us)
Async XLA Ops:
  6.5 9.0 %copy-start = (bf16[2,16]{1,0:T(2,128)(2,1)S(1)}, bf16[2,16]{1,0:T(2,128)(2,1)}, u32[]{:S(2)}) copy-start(bf16[2,16]{1,0:T(2,128)(2,1)} %param.6) | copy-start | bytes 196
  6.5 85.5 %all-gather.5.cloned.1.call-start = ((), (), s32[]{:S(2)}) async-start(), calls=%async_computation.2 | async-start | bytes 2359296 | tf_op jit(solution)/shard_map/all_gather | solution.py:186
  7.5 14.6 %collective-permute-start.1 = (bf16[3,64,512]{2,1,0:T(8,128)(2,1)S(1)}, bf16[3,64,512]{2,1,0:T(8,128)(2,1)S(1)}, u32[]{:S(2)}, u32[]{:S(2)}) collective-permute-start(bf16[3,64,512]{2,1,0:T(8,128)(2,1)S(1)} %constant_dynamic-slice_fusion), channel_id=1, source_target_pairs={{0,64},{64,128},{128,192},{192,0},{1,65},{65,129},{129,193},{193,1... | collective-permute-start | bytes 589832 | tf_op jit(solution)/shard_map/ppermute | solution.py:46
  9.1 13.0 %collective-permute-start.2 = (bf16[3,64,512]{2,1,0:T(8,128)(2,1)S(1)}, bf16[3,64,512]{2,1,0:T(8,128)(2,1)S(1)}, u32[]{:S(2)}, u32[]{:S(2)}) collective-permute-start(bf16[3,64,512]{2,1,0:T(8,128)(2,1)S(1)} %constant_dynamic-slice_fusion), channel_id=1, source_target_pairs={{0,128},{64,192},{128,0},{192,64},{1,129},{65,193},{129,1},{193,65... | collective-permute-start | bytes 589832 | tf_op jit(solution)/shard_map/ppermute | solution.py:46
  11.8 10.3 %collective-permute-start.3 = (bf16[3,64,512]{2,1,0:T(8,128)(2,1)S(1)}, bf16[3,64,512]{2,1,0:T(8,128)(2,1)S(1)}, u32[]{:S(2)}, u32[]{:S(2)}) collective-permute-start(bf16[3,64,512]{2,1,0:T(8,128)(2,1)S(1)} %constant_dynamic-slice_fusion), channel_id=1, source_target_pairs={{0,192},{64,0},{128,64},{192,128},{1,193},{65,1},{129,65},{193,129... | collective-permute-start | bytes 589832 | tf_op jit(solution)/shard_map/ppermute | solution.py:46
  14.1 7.1 %collective-permute-start = (bf16[64,512]{1,0:T(8,128)(2,1)S(1)}, bf16[64,512]{1,0:T(8,128)(2,1)S(1)}, u32[]{:S(2)}, u32[]{:S(2)}) collective-permute-start(bf16[64,512]{1,0:T(8,128)(2,1)S(1)} %dynamic-slice_bitcast_fusion), channel_id=1, source_target_pairs={{0,8},{1,9},{2,10},{3,11},{4,12},{5,13},{6,14},{7,15},{8,0},{9,1},... | collective-permute-start | bytes 196616 | tf_op jit(solution)/shard_map/ppermute | solution.py:41
  21.1 3.3 %copy-start.13 = (s32[4,256]{1,0:T(4,128)S(1)}, s32[4,256]{1,0:T(4,128)}, u32[]{:S(2)}) copy-start(s32[4,256]{1,0:T(4,128)} %param.9) | copy-start | bytes 12292
  22.1 2.9 %copy-start.4 = (bf16[3,64,512]{2,1,0:T(8,128)(2,1)}, bf16[3,64,512]{2,1,0:T(8,128)(2,1)S(1)}, u32[]{:S(2)}) copy-start(bf16[3,64,512]{2,1,0:T(8,128)(2,1)S(1)} %collective-permute-done.1) | copy-start | bytes 589828
  22.1 2.9 %copy-start.6 = (bf16[3,64,512]{2,1,0:T(8,128)(2,1)}, bf16[3,64,512]{2,1,0:T(8,128)(2,1)S(1)}, u32[]{:S(2)}) copy-start(bf16[3,64,512]{2,1,0:T(8,128)(2,1)S(1)} %collective-permute-done.2) | copy-start | bytes 589828
  22.1 2.9 %copy-start.8 = (bf16[3,64,512]{2,1,0:T(8,128)(2,1)}, bf16[3,64,512]{2,1,0:T(8,128)(2,1)S(1)}, u32[]{:S(2)}) copy-start(bf16[3,64,512]{2,1,0:T(8,128)(2,1)S(1)} %collective-permute-done.3) | copy-start | bytes 589828
  23.8 9.2 %collective-permute-start.4 = (bf16[128,512]{1,0:T(8,128)(2,1)S(1)}, bf16[128,512]{1,0:T(8,128)(2,1)S(1)}, u32[]{:S(2)}, u32[]{:S(2)}) collective-permute-start(bf16[128,512]{1,0:T(8,128)(2,1)S(1)} %pad_maximum_fusion.8), channel_id=1, source_target_pairs={{0,16},{1,17},{2,18},{3,19},{4,20},{5,21},{6,22},{7,23},{8,24},{9,... | collective-permute-start | bytes 393224 | tf_op jit(solution)/shard_map/ppermute | solution.py:41
  25.0 24.4 %all-to-all-start = ((bf16[8,512,128]{2,1,0:T(8,128)(2,1)}), bf16[8,512,128]{2,1,0:T(8,128)(2,1)S(1)}, u32[]{:S(2)}, u32[]{:S(2)}) async-start(bf16[8,512,128]{2,1,0:T(8,128)(2,1)} %bitcast.5), calls=%async_computation | async-start | bytes 2097152 | tf_op jit(solution)/shard_map/all_to_all | solution.py:176
  29.5 118.8 %all-gather.7.cloned.1.call-start = ((), (), s32[]{:S(2)}) async-start(), calls=%async_computation.3 | async-start | bytes 4718592 | tf_op jit(solution)/shard_map/all_gather | solution.py:191
  29.5 6.8 %copy-start.5 = (bf16[3,64,512]{2,1,0:T(8,128)(2,1)S(1)}, bf16[3,64,512]{2,1,0:T(8,128)(2,1)}, u32[]{:S(2)}) copy-start(bf16[3,64,512]{2,1,0:T(8,128)(2,1)} %copy-done.4) | copy-start | bytes 589828
  29.5 6.8 %copy-start.7 = (bf16[3,64,512]{2,1,0:T(8,128)(2,1)S(1)}, bf16[3,64,512]{2,1,0:T(8,128)(2,1)}, u32[]{:S(2)}) copy-start(bf16[3,64,512]{2,1,0:T(8,128)(2,1)} %copy-done.6) | copy-start | bytes 589828
  29.5 6.8 %copy-start.9 = (bf16[3,64,512]{2,1,0:T(8,128)(2,1)S(1)}, bf16[3,64,512]{2,1,0:T(8,128)(2,1)}, u32[]{:S(2)}) copy-start(bf16[3,64,512]{2,1,0:T(8,128)(2,1)} %copy-done.8) | copy-start | bytes 589828
  33.0 3.2 %copy-start.3 = (bf16[128,512]{1,0:T(8,128)(2,1)}, bf16[128,512]{1,0:T(8,128)(2,1)S(1)}, u32[]{:S(2)}) copy-start(bf16[128,512]{1,0:T(8,128)(2,1)S(1)} %get-tuple-element.64) | copy-start | bytes 393220
  33.8 14.5 %collective-permute-start.5 = (bf16[256,512]{1,0:T(8,128)(2,1)}, bf16[256,512]{1,0:T(8,128)(2,1)}, u32[]{:S(2)}, u32[]{:S(2)}) collective-permute-start(bf16[256,512]{1,0:T(8,128)(2,1)} %pad_maximum_fusion.7), channel_id=1, source_target_pairs={{0,32},{1,33},{2,34},{3,35},{4,36},{5,37},{6,38},{7,39},{8,40},{9,... | collective-permute-start | bytes 786440 | tf_op jit(solution)/shard_map/ppermute | solution.py:41
  50.3 16.1 %copy-start.14 = (s32[256]{0:T(256)S(1)}, s32[256]{0:T(256)}, u32[]{:S(2)}) copy-start(s32[256]{0:T(256)} %param.8) | copy-start | bytes 3076
  51.2 40.4 %all-to-all-start.1 = ((bf16[32,8,1024]{2,1,0:T(8,128)(2,1)}), bf16[32,8,1024]{2,1,0:T(8,128)(2,1)S(1)}, u32[]{:S(2)}, u32[]{:S(2)}) async-start(bf16[32,8,1024]{2,1,0:T(8,128)(2,1)} %bitcast.14), calls=%async_computation.1 | async-start | bytes 1048576 | tf_op jit(solution)/shard_map/all_to_all | solution.py:185
  60.7 19.7 %collective-permute-start.6 = (bf16[512,512]{1,0:T(8,128)(2,1)S(1)}, bf16[512,512]{1,0:T(8,128)(2,1)S(1)}, u32[]{:S(2)}, u32[]{:S(2)}) collective-permute-start(bf16[512,512]{1,0:T(8,128)(2,1)S(1)} %pad_maximum_fusion.5), channel_id=1, source_target_pairs={{0,64},{64,128},{128,192},{192,0},{1,65},{65,129},{129,193},{193,1... | collective-permute-start | bytes 1572872 | tf_op jit(solution)/shard_map/ppermute | solution.py:46
  62.2 27.8 %collective-permute-start.7 = (bf16[512,512]{1,0:T(8,128)(2,1)S(1)}, bf16[512,512]{1,0:T(8,128)(2,1)S(1)}, u32[]{:S(2)}, u32[]{:S(2)}) collective-permute-start(bf16[512,512]{1,0:T(8,128)(2,1)S(1)} %pad_maximum_fusion.5), channel_id=1, source_target_pairs={{0,128},{64,192},{128,0},{192,64},{1,129},{65,193},{129,1},{193,65... | collective-permute-start | bytes 1572872 | tf_op jit(solution)/shard_map/ppermute | solution.py:46
  64.9 25.0 %collective-permute-start.8 = (bf16[512,512]{1,0:T(8,128)(2,1)S(1)}, bf16[512,512]{1,0:T(8,128)(2,1)S(1)}, u32[]{:S(2)}, u32[]{:S(2)}) collective-permute-start(bf16[512,512]{1,0:T(8,128)(2,1)S(1)} %pad_maximum_fusion.5), channel_id=1, source_target_pairs={{0,192},{64,0},{128,64},{192,128},{1,193},{65,1},{129,65},{193,129... | collective-permute-start | bytes 1572872 | tf_op jit(solution)/shard_map/ppermute | solution.py:46
  92.0 4.8 %collective-permute-start.10 = (bf16[4,512,512]{2,1,0:T(8,128)(2,1)}, bf16[4,512,512]{2,1,0:T(8,128)(2,1)}, u32[]{:S(2)}, u32[]{:S(2)}) collective-permute-start(bf16[4,512,512]{2,1,0:T(8,128)(2,1)} %pad_maximum_fusion.mine), channel_id=1, source_target_pairs={{0,1},{1,0},{2,3},{3,2},{4,5},{5,4},{6,7},{7,6},{8,9},{9,8},{10,11... | collective-permute-start | bytes 6291464 | tf_op jit(solution)/shard_map/ppermute | solution.py:41
  92.1 8.2 %collective-permute-start.9 = (bf16[256,1024]{1,0:T(8,128)(2,1)S(1)}, bf16[256,1024]{1,0:T(8,128)(2,1)S(1)}, u32[]{:S(2)}, u32[]{:S(2)}) collective-permute-start(bf16[256,1024]{1,0:T(8,128)(2,1)S(1)} %leaves.1.own), channel_id=1, source_target_pairs={{0,1},{1,0},{2,3},{3,2},{4,5},{5,4},{6,7},{7,6},{8,9},{9,8},{10,11... | collective-permute-start | bytes 1572872 | tf_op jit(solution)/shard_map/ppermute | solution.py:41
  100.3 4.5 %copy-start.12 = (s32[256,1]{0,1:T(1,128)S(1)}, s32[256,1]{0,1:T(1,128)}, u32[]{:S(2)}) copy-start(s32[256,1]{0,1:T(1,128)} %get-tuple-element.37) | copy-start | bytes 3076
  101.2 4.5 %collective-permute-start.12 = (bf16[8,4,64,512]{3,2,1,0:T(8,128)(2,1)}, bf16[8,4,64,512]{3,2,1,0:T(8,128)(2,1)S(1)}, u32[]{:S(2)}, u32[]{:S(2)}) collective-permute-start(bf16[8,4,64,512]{3,2,1,0:T(8,128)(2,1)} %bitcast.24.mine), channel_id=1, source_target_pairs={{0,1},{1,0},{2,3},{3,2},{4,5},{5,4},{6,7},{7,6},{8,9},{9,8},{10,11... | collective-permute-start | bytes 6291464 | tf_op jit(solution)/shard_map/ppermute | solution.py:41
  101.4 15.8 %collective-permute-start.11 = (bf16[256,1024]{1,0:T(8,128)(2,1)S(1)}, bf16[256,1024]{1,0:T(8,128)(2,1)S(1)}, u32[]{:S(2)}, u32[]{:S(2)}) collective-permute-start(bf16[256,1024]{1,0:T(8,128)(2,1)S(1)} %far0.1.own), channel_id=1, source_target_pairs={{0,4},{1,5},{2,6},{3,7},{4,0},{5,1},{6,2},{7,3},{8,12},{9,13},{10,... | collective-permute-start | bytes 1572872 | tf_op jit(solution)/shard_map/ppermute | solution.py:41
  105.7 1.4 copy-start.2
  117.2 1.9 %copy-start.11 = (s32[256,1]{0,1:T(1,128)S(1)}, s32[256,1]{0,1:T(1,128)}, u32[]{:S(2)}) copy-start(s32[256,1]{0,1:T(1,128)} %get-tuple-element.36) | copy-start | bytes 3076
  118.1 30.2 %collective-permute-start.13 = (bf16[256,1024]{1,0:T(8,128)(2,1)S(1)}, bf16[256,1024]{1,0:T(8,128)(2,1)S(1)}, u32[]{:S(2)}, u32[]{:S(2)}) collective-permute-start(bf16[256,1024]{1,0:T(8,128)(2,1)S(1)} %far1.1.own), channel_id=1, source_target_pairs={{0,16},{1,17},{2,18},{3,19},{4,20},{5,21},{6,22},{7,23},{8,24},{9,... | collective-permute-start | bytes 1572872 | tf_op jit(solution)/shard_map/ppermute | solution.py:41
  148.2 7.4 %collective-permute-start.14 = (bf16[8,4,2,64,512]{4,3,2,1,0:T(8,128)(2,1)}, bf16[8,4,2,64,512]{4,3,2,1,0:T(8,128)(2,1)S(1)}, u32[]{:S(2)}, u32[]{:S(2)}) collective-permute-start(bf16[8,4,2,64,512]{4,3,2,1,0:T(8,128)(2,1)} %bitcast.46), channel_id=1, source_target_pairs={{0,1},{1,0},{2,3},{3,2},{4,5},{5,4},{6,7},{7,6},{8,9},{9,8},{10,11... | collective-permute-start | bytes 12582920 | tf_op jit(solution)/shard_map/ppermute | solution.py:41
  155.6 2.0 %copy-start.1 = (bf16[8,4,2,64,512]{4,3,2,1,0:T(8,128)(2,1)}, bf16[8,4,2,64,512]{4,3,2,1,0:T(8,128)(2,1)S(1)}, u32[]{:S(2)}) copy-start(bf16[8,4,2,64,512]{4,3,2,1,0:T(8,128)(2,1)S(1)} %collective-permute-done.14.other) | copy-start | bytes 12582916
  161.7 2.5 %copy-start.10 = (s32[256,1]{0,1:T(1,128)S(1)}, s32[256,1]{0,1:T(1,128)}, u32[]{:S(2)}) copy-start(s32[256,1]{0,1:T(1,128)} %get-tuple-element.35) | copy-start | bytes 3076
  162.6 14.1 %collective-permute-start.15 = (bf16[256,1024]{1,0:T(8,128)(2,1)S(1)}, bf16[256,1024]{1,0:T(8,128)(2,1)S(1)}, u32[]{:S(2)}, u32[]{:S(2)}) collective-permute-start(bf16[256,1024]{1,0:T(8,128)(2,1)S(1)} %far2.1.own), channel_id=1, source_target_pairs={{0,64},{1,65},{2,66},{3,67},{4,68},{5,69},{6,70},{7,71},{8,72},{9,... | collective-permute-start | bytes 1572872 | tf_op jit(solution)/shard_map/ppermute | solution.py:41
Sparse Core Ops, SparseCore 0:
  23.2 47.0 all-gather.4
  72.0 76.1 all-gather.6

commit v4 on v3

--- a/solution.py
+++ b/solution.py
@@ -105,10 +105,6 @@
         out[:, cols] = (total + partial[:, cols]).astype(BF16)
 
 
-def copy_body(values, out):
-    out[...] = values[...]
-
-
 def select_body(index, values, out):
     out[...] = select_rows(index[...], values[...])
 
@@ -199,8 +195,6 @@
             states, w23 = together((states, w23))
             others[2] = others[3] = flip(w23, 1)
         joined, partial = near_step(level, place, states, (w0, w1, w23, w23)[level], others[level])
-        if level == 2:
-            far = on_chip(copy_body, far.shape, LONG, "arrived2", far)
         states = far_step(level, pair_index[level], far, joined, partial)
     return states
 

time: 186 us -> 183 us (0.984)
  the two profiles are of different devices: /device:TPU:128 before, /device:TPU:2 now
where the time goes in v4:
time: 183 us
  waiting for transfers between devices  88.2 us (48%)
  starting transfers between devices  41.5 us (23%)
  Pallas kernels  21.1 us (12%)
  between operations  13.8 us (8%)
  other arithmetic  7 us (4%)
  matrix products  5.58 us (3%)
  local copies, waits for them, and re-layouts  5.57 us (3%)
    ppermute x10, waiting for transfers between devices, flip(): return lax.ppermute(value, AXES, [(i, i ^ mask) for i in range(size)])  53.5 us
    ppermute x6, waiting for transfers between devices, shifted(): return lax.ppermute(value, axis, [(i, (i + k) % size) for i in range(size)])  24.5 us
    ppermute x10, starting transfers between devices, flip(): return lax.ppermute(value, AXES, [(i, i ^ mask) for i in range(size)])  18.8 us
    pallas_call x4, Pallas kernels, near_step(): pl.pallas_call(functools.partial(near_body, level), out_shape=[jax.ShapeD...  15.7 us
    all_gather x1, waiting for transfers between devices, on_device(): w23 = lax.all_gather(late[:, 1:], ('zh', 'zl'))  10.1 us
    ppermute x6, starting transfers between devices, shifted(): return lax.ppermute(value, axis, [(i, (i + k) % size) for i in range(size)])  9.65 us
    all_to_all x1, starting transfers between devices, on_device(): lax.all_to_all(points, GROUP, split_axis=0, concat_axis=0, tiled=True)  8.57 us
    dot_general x1, matrix products, on_device(): jnp.einsum('cb,kbt->kct', interp, traces.reshape(local_boxes, BOXT, local...  5.58 us
  transfers between devices with their start and end apart: 20, of which 11 were waited for; matrix products, arithmetic and copies ran while one was open for 8% of the time, Pallas kernels for 10%

profile of v4, /device:TPU:2, one launch (start us, length us, event | category | flops | bytes accessed | tf_op | source)
XLA Modules:
  0.0 182.7 jit_solution(8167536053029692626)
XLA Ops:
  6.5 1.0 constant_dynamic-slice_fusion
  7.5 1.6 collective-permute-start.1
  9.1 2.8 %collective-permute-start.2 = (bf16[3,64,512]{2,1,0:T(8,128)(2,1)S(1)}, bf16[3,64,512]{2,1,0:T(8,128)(2,1)S(1)}, u32[]{:S(2)}, u32[]{:S(2)}) collective-permute-start(bf16[3,64,512]{2,1,0:T(8,128)(2,1)S(1)} %constant_dynamic-slice_fusion), channel_id=1, source_target_pairs={{0,128},{64,192},{128,0},{192,64},{1,129},{65,193},{129,1},{193,65... | collective-permute-start | bytes 589832 | tf_op jit(solution)/shard_map/ppermute | solution.py:46
  11.9 0.4 collective-permute-start.3
  12.3 0.8 dynamic-slice_bitcast_fusion
  13.2 3.3 %collective-permute-start = (bf16[64,512]{1,0:T(8,128)(2,1)S(1)}, bf16[64,512]{1,0:T(8,128)(2,1)S(1)}, u32[]{:S(2)}, u32[]{:S(2)}) collective-permute-start(bf16[64,512]{1,0:T(8,128)(2,1)S(1)} %dynamic-slice_bitcast_fusion), channel_id=1, source_target_pairs={{0,8},{1,9},{2,10},{3,11},{4,12},{5,13},{6,14},{7,15},{8,0},{9,1},... | collective-permute-start | bytes 196616 | tf_op jit(solution)/shard_map/ppermute | solution.py:41
  16.4 5.6 %convolution_convert_fusion = bf16[2048,128,2]{1,2,0:T(2,128)(2,1)} fusion(bf16[2048,16,128]{2,1,0:T(8,128)(2,1)} %bitcast.45, bf16[2,16]{1,0:T(2,128)(2,1)S(1)} %copy-done), kind=kOutput, calls=%fused_computation.1 | convolution fusion | flops 17301504 | bytes 9437248 | tf_op jit(solution)/shard_map/cb,kbt->kct/dot_general | solution.py:165
  22.0 0.9 broadcast_select_fusion.5
  23.0 0.9 pad_maximum_fusion.6
  24.3 0.4 subtract_convert_fusion
  24.6 5.5 %collective-permute-start.4 = (bf16[128,512]{1,0:T(8,128)(2,1)S(1)}, bf16[128,512]{1,0:T(8,128)(2,1)S(1)}, u32[]{:S(2)}, u32[]{:S(2)}) collective-permute-start(bf16[128,512]{1,0:T(8,128)(2,1)S(1)} %pad_maximum_fusion.8), channel_id=1, source_target_pairs={{0,16},{1,17},{2,18},{3,19},{4,20},{5,21},{6,22},{7,23},{8,24},{9,... | collective-permute-start | bytes 393224 | tf_op jit(solution)/shard_map/ppermute | solution.py:41
  30.1 0.5 slice_bitcast_fusion
  30.7 4.5 %all-to-all-start = ((bf16[8,512,128]{2,1,0:T(8,128)(2,1)}), bf16[8,512,128]{2,1,0:T(8,128)(2,1)S(1)}, u32[]{:S(2)}, u32[]{:S(2)}) async-start(bf16[8,512,128]{2,1,0:T(8,128)(2,1)} %bitcast.5), calls=%async_computation | async-start | bytes 2097152 | tf_op jit(solution)/shard_map/all_to_all | solution.py:172
  35.3 0.7 pad_maximum_fusion.7
  36.0 2.2 %collective-permute-start.5 = (bf16[256,512]{1,0:T(8,128)(2,1)}, bf16[256,512]{1,0:T(8,128)(2,1)}, u32[]{:S(2)}, u32[]{:S(2)}) collective-permute-start(bf16[256,512]{1,0:T(8,128)(2,1)} %pad_maximum_fusion.7), channel_id=1, source_target_pairs={{0,32},{1,33},{2,34},{3,35},{4,36},{5,37},{6,38},{7,39},{8,40},{9,... | collective-permute-start | bytes 786440 | tf_op jit(solution)/shard_map/ppermute | solution.py:41
  38.4 0.9 pad_maximum_fusion.2
  39.2 11.6 %collective-permute-done.5 = bf16[256,512]{1,0:T(8,128)(2,1)} collective-permute-done((bf16[256,512]{1,0:T(8,128)(2,1)}, bf16[256,512]{1,0:T(8,128)(2,1)}, u32[]{:S(2)}, u32[]{:S(2)}) %collective-permute-start.5) | collective-permute-done | bytes 262176 | tf_op jit(solution)/shard_map/ppermute | solution.py:41
  50.9 1.1 broadcast_select_fusion.1
  52.2 0.7 spectrum.1
  52.9 1.0 reshape.143
  53.9 8.6 %all-to-all-start.1 = ((bf16[32,8,1024]{2,1,0:T(8,128)(2,1)}), bf16[32,8,1024]{2,1,0:T(8,128)(2,1)S(1)}, u32[]{:S(2)}, u32[]{:S(2)}) async-start(bf16[32,8,1024]{2,1,0:T(8,128)(2,1)} %bitcast.14), calls=%async_computation.1 | async-start | bytes 1048576 | tf_op jit(solution)/shard_map/all_to_all | solution.py:181
  62.5 1.5 collective-permute-start.6
  64.0 0.8 collective-permute-start.7
  64.8 2.4 %collective-permute-start.8 = (bf16[512,512]{1,0:T(8,128)(2,1)S(1)}, bf16[512,512]{1,0:T(8,128)(2,1)S(1)}, u32[]{:S(2)}, u32[]{:S(2)}) collective-permute-start(bf16[512,512]{1,0:T(8,128)(2,1)S(1)} %pad_maximum_fusion.5), channel_id=1, source_target_pairs={{0,192},{64,0},{128,64},{192,128},{1,193},{65,1},{129,65},{193,129... | collective-permute-start | bytes 1572872 | tf_op jit(solution)/shard_map/ppermute | solution.py:46
  67.4 14.0 %collective-permute-done.6 = bf16[512,512]{1,0:T(8,128)(2,1)S(1)} collective-permute-done((bf16[512,512]{1,0:T(8,128)(2,1)S(1)}, bf16[512,512]{1,0:T(8,128)(2,1)S(1)}, u32[]{:S(2)}, u32[]{:S(2)}) %collective-permute-start.6) | collective-permute-done | bytes 524320 | tf_op jit(solution)/shard_map/ppermute | solution.py:46
  81.4 3.0 %collective-permute-done.7 = bf16[512,512]{1,0:T(8,128)(2,1)S(1)} collective-permute-done((bf16[512,512]{1,0:T(8,128)(2,1)S(1)}, bf16[512,512]{1,0:T(8,128)(2,1)S(1)}, u32[]{:S(2)}, u32[]{:S(2)}) %collective-permute-start.7) | collective-permute-done | bytes 524320 | tf_op jit(solution)/shard_map/ppermute | solution.py:46
  84.4 7.5 %collective-permute-done.8 = bf16[512,512]{1,0:T(8,128)(2,1)S(1)} collective-permute-done((bf16[512,512]{1,0:T(8,128)(2,1)S(1)}, bf16[512,512]{1,0:T(8,128)(2,1)S(1)}, u32[]{:S(2)}, u32[]{:S(2)}) %collective-permute-start.8) | collective-permute-done | bytes 524320 | tf_op jit(solution)/shard_map/ppermute | solution.py:46
  91.9 1.7 pad_maximum_fusion.mine
  94.1 0.5 collective-permute-start.9
  94.8 4.0 %collective-permute-done.10.other = bf16[4,512,512]{2,1,0:T(8,128)(2,1)} collective-permute-done((bf16[4,512,512]{2,1,0:T(8,128)(2,1)}, bf16[4,512,512]{2,1,0:T(8,128)(2,1)}, u32[]{:S(2)}, u32[]{:S(2)}) %collective-permute-start.10) | collective-permute-done | bytes 2097184 | tf_op jit(solution)/shard_map/ppermute | solution.py:41
  98.7 3.5 %near0.1 = (bf16[2048,1024]{1,0:T(8,128)(2,1)S(1)}, f32[256,1024]{1,0:T(8,128)S(1)}) custom-call(s32[2]{0:T(128)S(1)} %pad_add_fusion.place, bf16[256,1024]{1,0:T(8,128)(2,1)S(1)} %leaves.1.own, bf16[4,512,512]{2,1,0:T(8,128)(2,1)} %pad_maximum_fusion.mine, bf16[4,512,512]{2,1,0:T(8,128)(2,1)} %collective-permute-done.10.other), custom_call_target="tpu_custom_call" | custom-call | flops 536870912 | bytes 6291456 | tf_op jit(solution)/shard_map/near0/pallas_call | solution.py:135
  102.3 0.9 far0.1.own
  103.4 3.3 %collective-permute-start.11 = (bf16[256,1024]{1,0:T(8,128)(2,1)S(1)}, bf16[256,1024]{1,0:T(8,128)(2,1)S(1)}, u32[]{:S(2)}, u32[]{:S(2)}) collective-permute-start(bf16[256,1024]{1,0:T(8,128)(2,1)S(1)} %far0.1.own), channel_id=1, source_target_pairs={{0,4},{1,5},{2,6},{3,7},{4,0},{5,1},{6,2},{7,3},{8,12},{9,13},{10,... | collective-permute-start | bytes 1572872 | tf_op jit(solution)/shard_map/ppermute | solution.py:41
  106.8 0.8 collective-permute-done.12.other
  107.6 1.4 copy-done.1
  109.0 4.1 %near1.1 = (bf16[2048,1024]{1,0:T(8,128)(2,1)S(1)}, f32[256,1024]{1,0:T(8,128)S(1)}) custom-call(s32[2]{0:T(128)S(1)} %pad_add_fusion.place, bf16[256,1024]{1,0:T(8,128)(2,1)S(1)} %far0.1.own, bf16[8,4,64,512]{3,2,1,0:T(8,128)(2,1)} %bitcast.24.mine, bf16[8,4,64,512]{3,2,1,0:T(8,128)(2,1)} %copy-done.1), custom_call_target="tpu_custom_call" | custom-call | flops 536870912 | bytes 6291456 | tf_op jit(solution)/shard_map/near1/pallas_call | solution.py:135
  113.1 6.0 %collective-permute-done.11.far = bf16[256,1024]{1,0:T(8,128)(2,1)S(1)} collective-permute-done((bf16[256,1024]{1,0:T(8,128)(2,1)S(1)}, bf16[256,1024]{1,0:T(8,128)(2,1)S(1)}, u32[]{:S(2)}, u32[]{:S(2)}) %collective-permute-start.11) | collective-permute-done | bytes 524320 | tf_op jit(solution)/shard_map/ppermute | solution.py:41
  119.1 0.9 far1.1.own
  120.0 10.1 %all-gather.7.cloned.1.call-done = bf16[32,2,64,512]{3,2,1,0:T(8,128)(2,1)} async-done(((bf16[4,2,64,512]{3,2,1,0:T(8,128)(2,1)}), bf16[32,2,64,512]{3,2,1,0:T(8,128)(2,1)}) %all-gather.7.cloned.1.call-update) | async-done | bytes 4194320 | tf_op jit(solution)/shard_map/all_gather | solution.py:187
  130.1 3.0 %collective-permute-start.13 = (bf16[256,1024]{1,0:T(8,128)(2,1)S(1)}, bf16[256,1024]{1,0:T(8,128)(2,1)S(1)}, u32[]{:S(2)}, u32[]{:S(2)}) collective-permute-start(bf16[256,1024]{1,0:T(8,128)(2,1)S(1)} %far1.1.own), channel_id=1, source_target_pairs={{0,16},{1,17},{2,18},{3,19},{4,20},{5,21},{6,22},{7,23},{8,24},{9,... | collective-permute-start | bytes 1572872 | tf_op jit(solution)/shard_map/ppermute | solution.py:41
  133.3 4.3 %collective-permute-done.14.other = bf16[8,4,2,64,512]{4,3,2,1,0:T(8,128)(2,1)} collective-permute-done((bf16[8,4,2,64,512]{4,3,2,1,0:T(8,128)(2,1)}, bf16[8,4,2,64,512]{4,3,2,1,0:T(8,128)(2,1)}, u32[]{:S(2)}, u32[]{:S(2)}) %collective-permute-start.14) | collective-permute-done | bytes 4194336 | tf_op jit(solution)/shard_map/ppermute | solution.py:41
  137.6 4.0 %near2.1 = (bf16[2048,1024]{1,0:T(8,128)(2,1)S(1)}, f32[256,1024]{1,0:T(8,128)S(1)}) custom-call(s32[2]{0:T(128)S(1)} %pad_add_fusion.place, bf16[256,1024]{1,0:T(8,128)(2,1)S(1)} %far1.1.own, bf16[8,4,2,64,512]{4,3,2,1,0:T(8,128)(2,1)} %bitcast.47, bf16[8,4,2,64,512]{4,3,2,1,0:T(8,128)(2,1)} %collective-permute-done.14.other), custom_call_target="tpu_custom_call" | custom-call | flops 536870912 | bytes 6291456 | tf_op jit(solution)/shard_map/near2/pallas_call | solution.py:135
  141.6 18.1 %collective-permute-done.13.far = bf16[256,1024]{1,0:T(8,128)(2,1)S(1)} collective-permute-done((bf16[256,1024]{1,0:T(8,128)(2,1)S(1)}, bf16[256,1024]{1,0:T(8,128)(2,1)S(1)}, u32[]{:S(2)}, u32[]{:S(2)}) %collective-permute-start.13) | collective-permute-done | bytes 524320 | tf_op jit(solution)/shard_map/ppermute | solution.py:41
  159.7 0.9 far2.1.own
  160.6 0.6 collective-permute-start.15
  161.4 4.0 %near3.1 = (bf16[2048,1024]{1,0:T(8,128)(2,1)S(1)}, f32[256,1024]{1,0:T(8,128)S(1)}) custom-call(s32[2]{0:T(128)S(1)} %pad_add_fusion.place, bf16[256,1024]{1,0:T(8,128)(2,1)S(1)} %far2.1.own, bf16[8,4,2,64,512]{4,3,2,1,0:T(8,128)(2,1)} %bitcast.48, bf16[8,4,2,64,512]{4,3,2,1,0:T(8,128)(2,1)} %collective-permute-done.14.other), custom_call_target="tpu_custom_call" | custom-call | flops 536870912 | bytes 6291456 | tf_op jit(solution)/shard_map/near3/pallas_call | solution.py:135
  165.5 8.7 %collective-permute-done.15.far = bf16[256,1024]{1,0:T(8,128)(2,1)S(1)} collective-permute-done((bf16[256,1024]{1,0:T(8,128)(2,1)S(1)}, bf16[256,1024]{1,0:T(8,128)(2,1)S(1)}, u32[]{:S(2)}, u32[]{:S(2)}) %collective-permute-start.15) | collective-permute-done | bytes 524320 | tf_op jit(solution)/shard_map/ppermute | solution.py:41
  174.2 1.7 far3.1
  (58 shorter events, 2.2 us)
Async XLA Ops:
  6.5 9.9 %copy-start = (bf16[2,16]{1,0:T(2,128)(2,1)S(1)}, bf16[2,16]{1,0:T(2,128)(2,1)}, u32[]{:S(2)}) copy-start(bf16[2,16]{1,0:T(2,128)(2,1)} %param.6) | copy-start | bytes 196
  6.5 87.4 %all-gather.5.cloned.1.call-start = ((), (), s32[]{:S(2)}) async-start(), calls=%async_computation.2 | async-start | bytes 2359296 | tf_op jit(solution)/shard_map/all_gather | solution.py:182
  7.5 15.4 %collective-permute-start.1 = (bf16[3,64,512]{2,1,0:T(8,128)(2,1)S(1)}, bf16[3,64,512]{2,1,0:T(8,128)(2,1)S(1)}, u32[]{:S(2)}, u32[]{:S(2)}) collective-permute-start(bf16[3,64,512]{2,1,0:T(8,128)(2,1)S(1)} %constant_dynamic-slice_fusion), channel_id=1, source_target_pairs={{0,64},{64,128},{128,192},{192,0},{1,65},{65,129},{129,193},{193,1... | collective-permute-start | bytes 589832 | tf_op jit(solution)/shard_map/ppermute | solution.py:46
  9.1 13.9 %collective-permute-start.2 = (bf16[3,64,512]{2,1,0:T(8,128)(2,1)S(1)}, bf16[3,64,512]{2,1,0:T(8,128)(2,1)S(1)}, u32[]{:S(2)}, u32[]{:S(2)}) collective-permute-start(bf16[3,64,512]{2,1,0:T(8,128)(2,1)S(1)} %constant_dynamic-slice_fusion), channel_id=1, source_target_pairs={{0,128},{64,192},{128,0},{192,64},{1,129},{65,193},{129,1},{193,65... | collective-permute-start | bytes 589832 | tf_op jit(solution)/shard_map/ppermute | solution.py:46
  11.9 11.1 %collective-permute-start.3 = (bf16[3,64,512]{2,1,0:T(8,128)(2,1)S(1)}, bf16[3,64,512]{2,1,0:T(8,128)(2,1)S(1)}, u32[]{:S(2)}, u32[]{:S(2)}) collective-permute-start(bf16[3,64,512]{2,1,0:T(8,128)(2,1)S(1)} %constant_dynamic-slice_fusion), channel_id=1, source_target_pairs={{0,192},{64,0},{128,64},{192,128},{1,193},{65,1},{129,65},{193,129... | collective-permute-start | bytes 589832 | tf_op jit(solution)/shard_map/ppermute | solution.py:46
  13.2 8.9 %collective-permute-start = (bf16[64,512]{1,0:T(8,128)(2,1)S(1)}, bf16[64,512]{1,0:T(8,128)(2,1)S(1)}, u32[]{:S(2)}, u32[]{:S(2)}) collective-permute-start(bf16[64,512]{1,0:T(8,128)(2,1)S(1)} %dynamic-slice_bitcast_fusion), channel_id=1, source_target_pairs={{0,8},{1,9},{2,10},{3,11},{4,12},{5,13},{6,14},{7,15},{8,0},{9,1},... | collective-permute-start | bytes 196616 | tf_op jit(solution)/shard_map/ppermute | solution.py:41
  22.0 8.1 %copy-start.12 = (s32[4,256]{1,0:T(4,128)S(1)}, s32[4,256]{1,0:T(4,128)}, u32[]{:S(2)}) copy-start(s32[4,256]{1,0:T(4,128)} %param.9) | copy-start | bytes 12292
  22.9 7.7 %copy-start.3 = (bf16[3,64,512]{2,1,0:T(8,128)(2,1)}, bf16[3,64,512]{2,1,0:T(8,128)(2,1)S(1)}, u32[]{:S(2)}) copy-start(bf16[3,64,512]{2,1,0:T(8,128)(2,1)S(1)} %collective-permute-done.1) | copy-start | bytes 589828
  23.0 7.7 %copy-start.5 = (bf16[3,64,512]{2,1,0:T(8,128)(2,1)}, bf16[3,64,512]{2,1,0:T(8,128)(2,1)S(1)}, u32[]{:S(2)}) copy-start(bf16[3,64,512]{2,1,0:T(8,128)(2,1)S(1)} %collective-permute-done.2) | copy-start | bytes 589828
  23.0 7.7 %copy-start.7 = (bf16[3,64,512]{2,1,0:T(8,128)(2,1)}, bf16[3,64,512]{2,1,0:T(8,128)(2,1)S(1)}, u32[]{:S(2)}) copy-start(bf16[3,64,512]{2,1,0:T(8,128)(2,1)S(1)} %collective-permute-done.3) | copy-start | bytes 589828
  24.6 10.6 %collective-permute-start.4 = (bf16[128,512]{1,0:T(8,128)(2,1)S(1)}, bf16[128,512]{1,0:T(8,128)(2,1)S(1)}, u32[]{:S(2)}, u32[]{:S(2)}) collective-permute-start(bf16[128,512]{1,0:T(8,128)(2,1)S(1)} %pad_maximum_fusion.8), channel_id=1, source_target_pairs={{0,16},{1,17},{2,18},{3,19},{4,20},{5,21},{6,22},{7,23},{8,24},{9,... | collective-permute-start | bytes 393224 | tf_op jit(solution)/shard_map/ppermute | solution.py:41
  30.7 21.3 %all-to-all-start = ((bf16[8,512,128]{2,1,0:T(8,128)(2,1)}), bf16[8,512,128]{2,1,0:T(8,128)(2,1)S(1)}, u32[]{:S(2)}, u32[]{:S(2)}) async-start(bf16[8,512,128]{2,1,0:T(8,128)(2,1)} %bitcast.5), calls=%async_computation | async-start | bytes 2097152 | tf_op jit(solution)/shard_map/all_to_all | solution.py:172
  35.2 94.9 %all-gather.7.cloned.1.call-start = ((), (), s32[]{:S(2)}) async-start(), calls=%async_computation.3 | async-start | bytes 4718592 | tf_op jit(solution)/shard_map/all_gather | solution.py:187
  35.2 3.1 %copy-start.4 = (bf16[3,64,512]{2,1,0:T(8,128)(2,1)S(1)}, bf16[3,64,512]{2,1,0:T(8,128)(2,1)}, u32[]{:S(2)}) copy-start(bf16[3,64,512]{2,1,0:T(8,128)(2,1)} %copy-done.3) | copy-start | bytes 589828
  35.2 3.1 %copy-start.6 = (bf16[3,64,512]{2,1,0:T(8,128)(2,1)S(1)}, bf16[3,64,512]{2,1,0:T(8,128)(2,1)}, u32[]{:S(2)}) copy-start(bf16[3,64,512]{2,1,0:T(8,128)(2,1)} %copy-done.5) | copy-start | bytes 589828
  35.2 3.1 %copy-start.8 = (bf16[3,64,512]{2,1,0:T(8,128)(2,1)S(1)}, bf16[3,64,512]{2,1,0:T(8,128)(2,1)}, u32[]{:S(2)}) copy-start(bf16[3,64,512]{2,1,0:T(8,128)(2,1)} %copy-done.7) | copy-start | bytes 589828
  35.3 3.0 %copy-start.2 = (bf16[128,512]{1,0:T(8,128)(2,1)}, bf16[128,512]{1,0:T(8,128)(2,1)S(1)}, u32[]{:S(2)}) copy-start(bf16[128,512]{1,0:T(8,128)(2,1)S(1)} %get-tuple-element.64) | copy-start | bytes 393220
  36.0 14.9 %collective-permute-start.5 = (bf16[256,512]{1,0:T(8,128)(2,1)}, bf16[256,512]{1,0:T(8,128)(2,1)}, u32[]{:S(2)}, u32[]{:S(2)}) collective-permute-start(bf16[256,512]{1,0:T(8,128)(2,1)} %pad_maximum_fusion.7), channel_id=1, source_target_pairs={{0,32},{1,33},{2,34},{3,35},{4,36},{5,37},{6,38},{7,39},{8,40},{9,... | collective-permute-start | bytes 786440 | tf_op jit(solution)/shard_map/ppermute | solution.py:41
  52.9 14.4 %copy-start.13 = (s32[256]{0:T(256)S(1)}, s32[256]{0:T(256)}, u32[]{:S(2)}) copy-start(s32[256]{0:T(256)} %param.8) | copy-start | bytes 3076
  53.9 39.7 %all-to-all-start.1 = ((bf16[32,8,1024]{2,1,0:T(8,128)(2,1)}), bf16[32,8,1024]{2,1,0:T(8,128)(2,1)S(1)}, u32[]{:S(2)}, u32[]{:S(2)}) async-start(bf16[32,8,1024]{2,1,0:T(8,128)(2,1)} %bitcast.14), calls=%async_computation.1 | async-start | bytes 1048576 | tf_op jit(solution)/shard_map/all_to_all | solution.py:181
  62.5 19.0 %collective-permute-start.6 = (bf16[512,512]{1,0:T(8,128)(2,1)S(1)}, bf16[512,512]{1,0:T(8,128)(2,1)S(1)}, u32[]{:S(2)}, u32[]{:S(2)}) collective-permute-start(bf16[512,512]{1,0:T(8,128)(2,1)S(1)} %pad_maximum_fusion.5), channel_id=1, source_target_pairs={{0,64},{64,128},{128,192},{192,0},{1,65},{65,129},{129,193},{193,1... | collective-permute-start | bytes 1572872 | tf_op jit(solution)/shard_map/ppermute | solution.py:46
  64.0 20.4 %collective-permute-start.7 = (bf16[512,512]{1,0:T(8,128)(2,1)S(1)}, bf16[512,512]{1,0:T(8,128)(2,1)S(1)}, u32[]{:S(2)}, u32[]{:S(2)}) collective-permute-start(bf16[512,512]{1,0:T(8,128)(2,1)S(1)} %pad_maximum_fusion.5), channel_id=1, source_target_pairs={{0,128},{64,192},{128,0},{192,64},{1,129},{65,193},{129,1},{193,65... | collective-permute-start | bytes 1572872 | tf_op jit(solution)/shard_map/ppermute | solution.py:46
  64.8 27.1 %collective-permute-start.8 = (bf16[512,512]{1,0:T(8,128)(2,1)S(1)}, bf16[512,512]{1,0:T(8,128)(2,1)S(1)}, u32[]{:S(2)}, u32[]{:S(2)}) collective-permute-start(bf16[512,512]{1,0:T(8,128)(2,1)S(1)} %pad_maximum_fusion.5), channel_id=1, source_target_pairs={{0,192},{64,0},{128,64},{192,128},{1,193},{65,1},{129,65},{193,129... | collective-permute-start | bytes 1572872 | tf_op jit(solution)/shard_map/ppermute | solution.py:46
  94.0 4.8 %collective-permute-start.10 = (bf16[4,512,512]{2,1,0:T(8,128)(2,1)}, bf16[4,512,512]{2,1,0:T(8,128)(2,1)}, u32[]{:S(2)}, u32[]{:S(2)}) collective-permute-start(bf16[4,512,512]{2,1,0:T(8,128)(2,1)} %pad_maximum_fusion.mine), channel_id=1, source_target_pairs={{0,1},{1,0},{2,3},{3,2},{4,5},{5,4},{6,7},{7,6},{8,9},{9,8},{10,11... | collective-permute-start | bytes 6291464 | tf_op jit(solution)/shard_map/ppermute | solution.py:41
  94.1 8.2 %collective-permute-start.9 = (bf16[256,1024]{1,0:T(8,128)(2,1)S(1)}, bf16[256,1024]{1,0:T(8,128)(2,1)S(1)}, u32[]{:S(2)}, u32[]{:S(2)}) collective-permute-start(bf16[256,1024]{1,0:T(8,128)(2,1)S(1)} %leaves.1.own), channel_id=1, source_target_pairs={{0,1},{1,0},{2,3},{3,2},{4,5},{5,4},{6,7},{7,6},{8,9},{9,8},{10,11... | collective-permute-start | bytes 1572872 | tf_op jit(solution)/shard_map/ppermute | solution.py:41
  102.3 4.4 %copy-start.11 = (s32[256,1]{0,1:T(1,128)S(1)}, s32[256,1]{0,1:T(1,128)}, u32[]{:S(2)}) copy-start(s32[256,1]{0,1:T(1,128)} %get-tuple-element.37) | copy-start | bytes 3076
  103.2 4.5 %collective-permute-start.12 = (bf16[8,4,64,512]{3,2,1,0:T(8,128)(2,1)}, bf16[8,4,64,512]{3,2,1,0:T(8,128)(2,1)S(1)}, u32[]{:S(2)}, u32[]{:S(2)}) collective-permute-start(bf16[8,4,64,512]{3,2,1,0:T(8,128)(2,1)} %bitcast.24.mine), channel_id=1, source_target_pairs={{0,1},{1,0},{2,3},{3,2},{4,5},{5,4},{6,7},{7,6},{8,9},{9,8},{10,11... | collective-permute-start | bytes 6291464 | tf_op jit(solution)/shard_map/ppermute | solution.py:41
  103.4 15.7 %collective-permute-start.11 = (bf16[256,1024]{1,0:T(8,128)(2,1)S(1)}, bf16[256,1024]{1,0:T(8,128)(2,1)S(1)}, u32[]{:S(2)}, u32[]{:S(2)}) collective-permute-start(bf16[256,1024]{1,0:T(8,128)(2,1)S(1)} %far0.1.own), channel_id=1, source_target_pairs={{0,4},{1,5},{2,6},{3,7},{4,0},{5,1},{6,2},{7,3},{8,12},{9,13},{10,... | collective-permute-start | bytes 1572872 | tf_op jit(solution)/shard_map/ppermute | solution.py:41
  107.6 1.4 copy-start.1
  119.1 14.0 %copy-start.10 = (s32[256,1]{0,1:T(1,128)S(1)}, s32[256,1]{0,1:T(1,128)}, u32[]{:S(2)}) copy-start(s32[256,1]{0,1:T(1,128)} %get-tuple-element.36) | copy-start | bytes 3076
  130.1 7.5 %collective-permute-start.14 = (bf16[8,4,2,64,512]{4,3,2,1,0:T(8,128)(2,1)}, bf16[8,4,2,64,512]{4,3,2,1,0:T(8,128)(2,1)}, u32[]{:S(2)}, u32[]{:S(2)}) collective-permute-start(bf16[8,4,2,64,512]{4,3,2,1,0:T(8,128)(2,1)} %bitcast.46), channel_id=1, source_target_pairs={{0,1},{1,0},{2,3},{3,2},{4,5},{5,4},{6,7},{7,6},{8,9},{9,8},{10,11... | collective-permute-start | bytes 12582920 | tf_op jit(solution)/shard_map/ppermute | solution.py:41
  130.1 29.7 %collective-permute-start.13 = (bf16[256,1024]{1,0:T(8,128)(2,1)S(1)}, bf16[256,1024]{1,0:T(8,128)(2,1)S(1)}, u32[]{:S(2)}, u32[]{:S(2)}) collective-permute-start(bf16[256,1024]{1,0:T(8,128)(2,1)S(1)} %far1.1.own), channel_id=1, source_target_pairs={{0,16},{1,17},{2,18},{3,19},{4,20},{5,21},{6,22},{7,23},{8,24},{9,... | collective-permute-start | bytes 1572872 | tf_op jit(solution)/shard_map/ppermute | solution.py:41
  159.7 1.5 copy-start.9
  160.6 13.5 %collective-permute-start.15 = (bf16[256,1024]{1,0:T(8,128)(2,1)S(1)}, bf16[256,1024]{1,0:T(8,128)(2,1)S(1)}, u32[]{:S(2)}, u32[]{:S(2)}) collective-permute-start(bf16[256,1024]{1,0:T(8,128)(2,1)S(1)} %far2.1.own), channel_id=1, source_target_pairs={{0,64},{1,65},{2,66},{3,67},{4,68},{5,69},{6,70},{7,71},{8,72},{9,... | collective-permute-start | bytes 1572872 | tf_op jit(solution)/shard_map/ppermute | solution.py:41
Sparse Core Ops, SparseCore 0:
  24.0 50.5 all-gather.4
  76.4 53.5 all-gather.6
